TPU v7x, 256 devices: a whole 4x4x8 slice. The times are simulated.
256 devices in a mesh: tm: 32 (over y, z), cell: 8 (over x, core).
Axes of the slice: x: 4, y: 4, z: 8, core: 2. Of those that a mesh axis runs over, the one named last changes fastest.
Arguments:
- increments: int32 [768, 32768], P('cell', 'tm'), may hold values from 0 to 3
- noise: bfloat16 [768, 32768], P('cell', 'tm'), may hold values from -6 to 6
- noise_scale: float32 [768], P('cell'), may hold values from 0.5 to 4
- factor: bfloat16 [32768], replicated, may hold values from 0 to 2
Outputs:
- counts: int32 [768, 32768], P('cell', 'tm')
- correlated_noise: float32 [768, 32768], P('cell', 'tm')
- total_counts: int32 [32768], P('tm')
All inputs are finite; a program needn't handle non-finite values.
Results may differ from a plain program's by a relative error of at most 0.0009.
Values may be sent and summed in bfloat16 or wider, within the bound.
No kernel may reach another device: no remote copies, remote signals or barrier semaphores. Data moves between devices by JAX's collectives and lax.ppermute only.
A program may use at most 64 MiB of HBM per device.

v0:
```python
import jax
import jax.numpy as jnp
from jax import lax
from jax.sharding import PartitionSpec as P

BLK = 512


def prefix(value, axis, combine, identity):
    length, mine = (lax.axis_size(axis), lax.axis_index(axis))
    everything = lax.all_gather(value, axis)
    start = jnp.broadcast_to(jnp.asarray(identity, value.dtype), value.shape)

    def lap(k, before):
        reached = k < mine
        new = combine(before, everything[k])
        return jnp.where(reached, new, before)

    return lax.fori_loop(0, length, lap, start)


def toeplitz(padded, zero_pad, first_offset, rows_count, cols_count):
    period = rows_count + cols_count - 1
    forward_part = lax.dynamic_slice_in_dim(padded, zero_pad + first_offset, cols_count)
    behind = lax.dynamic_slice_in_dim(
        padded, zero_pad + first_offset - (rows_count - 1), rows_count - 1
    )
    pattern = jnp.concatenate([forward_part, behind])
    repeated = jnp.tile(pattern, rows_count)[: rows_count * (period - 1)]
    return repeated.reshape(rows_count, period - 1)[:, :cols_count]


def add_counts(earlier, later):
    return earlier + later


def shards(increments, noise, noise_scale, factor):
    local_sums = jnp.cumsum(increments, axis=1, dtype=jnp.int32)
    cells_here = increments.shape[0]
    carried = prefix(local_sums[:, -1], "tm", add_counts, jnp.zeros((cells_here,), jnp.int32))
    counts = local_sums + carried[:, None]
    group_sums = lax.all_gather(
        jnp.sum(counts, axis=0, dtype=jnp.int32)[None, :], "cell", axis=0, tiled=True
    )
    total_counts = jnp.sum(group_sums, axis=0, dtype=jnp.int32)
    zero_pad = factor.shape[0]
    padded = jnp.concatenate([jnp.zeros_like(factor), factor])
    position = lax.axis_index("tm")
    segment = noise.shape[1]
    block_len = BLK
    own_begin = position * segment
    empty_pair = (
        jnp.zeros((cells_here, segment), jnp.float32),
        jnp.zeros((cells_here, segment), jnp.float32),
    )
    pieces = lax.all_gather(noise, "tm", axis=1, tiled=True)

    def one_block(index_block, totals):
        own_acc, far_acc = totals
        source_begin = index_block * block_len
        source_block = lax.dynamic_slice_in_dim(pieces, index_block * block_len, block_len, 1)

        def product(target_begin):
            matrix = toeplitz(padded, zero_pad, target_begin - source_begin, block_len, segment)
            return jnp.dot(source_block, matrix, preferred_element_type=jnp.float32)

        def add_own(accum):
            return accum + product(own_begin)

        def keep_same(accum):
            return accum

        need_own = source_begin < own_begin + segment
        own_acc = lax.cond(need_own, add_own, keep_same, own_acc)
        return (own_acc, far_acc)

    own_acc, far_acc = lax.fori_loop(0, pieces.shape[1] // block_len, one_block, empty_pair)
    correlated_noise = noise_scale[:, None] * own_acc
    return (counts, correlated_noise, total_counts)


def solution(mesh):
    return jax.shard_map(
        shards,
        mesh=mesh,
        in_specs=(P("cell", "tm"), P("cell", "tm"), P("cell"), P()),
        out_specs=(P("cell", "tm"), P("cell", "tm"), P("tm")),
        check_vma=False,
    )
```

profile of v0, /device:TPU:249, one launch (start us, length us, event | category | flops | bytes accessed | tf_op | source)
XLA Modules:
  0.0 732.2 jit_solution(3635880137708631089)
XLA Ops:
  9.0 27.0 %reduce-window.6 = s32[96,8,128]{2,1,0:T(8,128)S(1)} reduce-window(s32[96,8,128]{2,1,0:T(8,128)S(1)} %bitcast.17, s32[]{:T(128)} %copy.32), window={size=1x1x128 pad=0_0x0_0x127_0}, to_apply=%region_0.0 | reduce-window | flops 12484608 | bytes 786436 | tf_op jit(solution)/shard_map/reduce-window
  38.4 111.0 %all-reduce.1 = s32[3072]{0:T(1024)S(1)} all-reduce(s32[3072]{0:T(1024)S(1)} %dynamic-update-slice), channel_id=2, replica_groups=mesh['tm'=32,'cell'=8] {'tm'}, use_global_device_ids=true, to_apply=%add.1 | all-reduce | flops 3072 | bytes 24576
  151.1 41.4 %all-gather.1 = s32[8,1,1024]{2,1,0:T(1,128)S(1)} all-gather(s32[1,1,1024]{2,1,0:T(1,128)S(1)} %bitcast.20), channel_id=1, replica_groups=mesh['tm'=32,'cell'=8] {'cell'}, dimensions={0}, use_global_device_ids=true | all-gather | bytes 36864 | tf_op jit(solution)/shard_map/all_gather | solution.py:42
  194.7 529.8 %while.31 = (s32[]{:T(128)}, f32[96,1024]{1,0:T(8,128)S(1)}, s32[]{:T(128)}, bf16[96,32768]{1,0:T(8,128)(2,1)}, s32[]{:T(128)}, /*index=5*/bf16[65536]{0:T(1024)(128)(2,1)}, s32[]{:T(128)}, s32[]{:T(128)}) while((s32[]{:T(128)}, f32[96,1024]{1,0:T(8,128)S(1)}, s32[]{:T(128)}, bf16[96,32768]{1,0:T(8,128)(2,1)}, s32[]{:T(128)}, ...), condition=%wide.region_7.8_spmd, body=%wide.region_4.7_spmd.sunk | while | flops 100767760 | bytes 12947755 | solution.py:77
  194.7 8.2 %conditional.2 = (f32[96,1024]{1,0:T(8,128)S(1)}) conditional(s32[]{:T(128)} %convert_element_type.9, f32[96,1024]{1,0:T(8,128)S(1)} %get-tuple-element.393, (s32[]{:T(128)}, bf16[96,32768]{1,0:T(8,128)(2,1)}, s32[]{:T(128)}, bf16[65536]{0:T(1024)(128)(2,1)}, f32[96,1024]{1,0:T(8,128)S(1)}) %tuple.80), branch_computations={%region_5.5_spmd, %region_6.6_spmd} | conditional | flops 100767752 | bytes 12947604 | solution.py:74
  203.0 8.2 %conditional.2 = (f32[96,1024]{1,0:T(8,128)S(1)}) conditional(s32[]{:T(128)} %convert_element_type.9, f32[96,1024]{1,0:T(8,128)S(1)} %get-tuple-element.393, (s32[]{:T(128)}, bf16[96,32768]{1,0:T(8,128)(2,1)}, s32[]{:T(128)}, bf16[65536]{0:T(1024)(128)(2,1)}, f32[96,1024]{1,0:T(8,128)S(1)}) %tuple.80), branch_computations={%region_5.5_spmd, %region_6.6_spmd} | conditional | flops 100767752 | bytes 12947604 | solution.py:74
  211.2 8.2 %conditional.2 = (f32[96,1024]{1,0:T(8,128)S(1)}) conditional(s32[]{:T(128)} %convert_element_type.9, f32[96,1024]{1,0:T(8,128)S(1)} %get-tuple-element.393, (s32[]{:T(128)}, bf16[96,32768]{1,0:T(8,128)(2,1)}, s32[]{:T(128)}, bf16[65536]{0:T(1024)(128)(2,1)}, f32[96,1024]{1,0:T(8,128)S(1)}) %tuple.80), branch_computations={%region_5.5_spmd, %region_6.6_spmd} | conditional | flops 100767752 | bytes 12947604 | solution.py:74
  219.5 8.2 %conditional.2 = (f32[96,1024]{1,0:T(8,128)S(1)}) conditional(s32[]{:T(128)} %convert_element_type.9, f32[96,1024]{1,0:T(8,128)S(1)} %get-tuple-element.393, (s32[]{:T(128)}, bf16[96,32768]{1,0:T(8,128)(2,1)}, s32[]{:T(128)}, bf16[65536]{0:T(1024)(128)(2,1)}, f32[96,1024]{1,0:T(8,128)S(1)}) %tuple.80), branch_computations={%region_5.5_spmd, %region_6.6_spmd} | conditional | flops 100767752 | bytes 12947604 | solution.py:74
  236.1 8.2 %conditional.2 = (f32[96,1024]{1,0:T(8,128)S(1)}) conditional(s32[]{:T(128)} %convert_element_type.9, f32[96,1024]{1,0:T(8,128)S(1)} %get-tuple-element.393, (s32[]{:T(128)}, bf16[96,32768]{1,0:T(8,128)(2,1)}, s32[]{:T(128)}, bf16[65536]{0:T(1024)(128)(2,1)}, f32[96,1024]{1,0:T(8,128)S(1)}) %tuple.80), branch_computations={%region_5.5_spmd, %region_6.6_spmd} | conditional | flops 100767752 | bytes 12947604 | solution.py:74
  244.4 8.2 %conditional.2 = (f32[96,1024]{1,0:T(8,128)S(1)}) conditional(s32[]{:T(128)} %convert_element_type.9, f32[96,1024]{1,0:T(8,128)S(1)} %get-tuple-element.393, (s32[]{:T(128)}, bf16[96,32768]{1,0:T(8,128)(2,1)}, s32[]{:T(128)}, bf16[65536]{0:T(1024)(128)(2,1)}, f32[96,1024]{1,0:T(8,128)S(1)}) %tuple.80), branch_computations={%region_5.5_spmd, %region_6.6_spmd} | conditional | flops 100767752 | bytes 12947604 | solution.py:74
  252.6 8.2 %conditional.2 = (f32[96,1024]{1,0:T(8,128)S(1)}) conditional(s32[]{:T(128)} %convert_element_type.9, f32[96,1024]{1,0:T(8,128)S(1)} %get-tuple-element.393, (s32[]{:T(128)}, bf16[96,32768]{1,0:T(8,128)(2,1)}, s32[]{:T(128)}, bf16[65536]{0:T(1024)(128)(2,1)}, f32[96,1024]{1,0:T(8,128)S(1)}) %tuple.80), branch_computations={%region_5.5_spmd, %region_6.6_spmd} | conditional | flops 100767752 | bytes 12947604 | solution.py:74
  269.2 8.2 %conditional.2 = (f32[96,1024]{1,0:T(8,128)S(1)}) conditional(s32[]{:T(128)} %convert_element_type.9, f32[96,1024]{1,0:T(8,128)S(1)} %get-tuple-element.393, (s32[]{:T(128)}, bf16[96,32768]{1,0:T(8,128)(2,1)}, s32[]{:T(128)}, bf16[65536]{0:T(1024)(128)(2,1)}, f32[96,1024]{1,0:T(8,128)S(1)}) %tuple.80), branch_computations={%region_5.5_spmd, %region_6.6_spmd} | conditional | flops 100767752 | bytes 12947604 | solution.py:74
  277.5 8.2 %conditional.2 = (f32[96,1024]{1,0:T(8,128)S(1)}) conditional(s32[]{:T(128)} %convert_element_type.9, f32[96,1024]{1,0:T(8,128)S(1)} %get-tuple-element.393, (s32[]{:T(128)}, bf16[96,32768]{1,0:T(8,128)(2,1)}, s32[]{:T(128)}, bf16[65536]{0:T(1024)(128)(2,1)}, f32[96,1024]{1,0:T(8,128)S(1)}) %tuple.80), branch_computations={%region_5.5_spmd, %region_6.6_spmd} | conditional | flops 100767752 | bytes 12947604 | solution.py:74
  285.7 8.2 %conditional.2 = (f32[96,1024]{1,0:T(8,128)S(1)}) conditional(s32[]{:T(128)} %convert_element_type.9, f32[96,1024]{1,0:T(8,128)S(1)} %get-tuple-element.393, (s32[]{:T(128)}, bf16[96,32768]{1,0:T(8,128)(2,1)}, s32[]{:T(128)}, bf16[65536]{0:T(1024)(128)(2,1)}, f32[96,1024]{1,0:T(8,128)S(1)}) %tuple.80), branch_computations={%region_5.5_spmd, %region_6.6_spmd} | conditional | flops 100767752 | bytes 12947604 | solution.py:74
  302.3 8.2 %conditional.2 = (f32[96,1024]{1,0:T(8,128)S(1)}) conditional(s32[]{:T(128)} %convert_element_type.9, f32[96,1024]{1,0:T(8,128)S(1)} %get-tuple-element.393, (s32[]{:T(128)}, bf16[96,32768]{1,0:T(8,128)(2,1)}, s32[]{:T(128)}, bf16[65536]{0:T(1024)(128)(2,1)}, f32[96,1024]{1,0:T(8,128)S(1)}) %tuple.80), branch_computations={%region_5.5_spmd, %region_6.6_spmd} | conditional | flops 100767752 | bytes 12947604 | solution.py:74
  310.6 8.2 %conditional.2 = (f32[96,1024]{1,0:T(8,128)S(1)}) conditional(s32[]{:T(128)} %convert_element_type.9, f32[96,1024]{1,0:T(8,128)S(1)} %get-tuple-element.393, (s32[]{:T(128)}, bf16[96,32768]{1,0:T(8,128)(2,1)}, s32[]{:T(128)}, bf16[65536]{0:T(1024)(128)(2,1)}, f32[96,1024]{1,0:T(8,128)S(1)}) %tuple.80), branch_computations={%region_5.5_spmd, %region_6.6_spmd} | conditional | flops 100767752 | bytes 12947604 | solution.py:74
  318.9 8.2 %conditional.2 = (f32[96,1024]{1,0:T(8,128)S(1)}) conditional(s32[]{:T(128)} %convert_element_type.9, f32[96,1024]{1,0:T(8,128)S(1)} %get-tuple-element.393, (s32[]{:T(128)}, bf16[96,32768]{1,0:T(8,128)(2,1)}, s32[]{:T(128)}, bf16[65536]{0:T(1024)(128)(2,1)}, f32[96,1024]{1,0:T(8,128)S(1)}) %tuple.80), branch_computations={%region_5.5_spmd, %region_6.6_spmd} | conditional | flops 100767752 | bytes 12947604 | solution.py:74
  335.4 8.2 %conditional.2 = (f32[96,1024]{1,0:T(8,128)S(1)}) conditional(s32[]{:T(128)} %convert_element_type.9, f32[96,1024]{1,0:T(8,128)S(1)} %get-tuple-element.393, (s32[]{:T(128)}, bf16[96,32768]{1,0:T(8,128)(2,1)}, s32[]{:T(128)}, bf16[65536]{0:T(1024)(128)(2,1)}, f32[96,1024]{1,0:T(8,128)S(1)}) %tuple.80), branch_computations={%region_5.5_spmd, %region_6.6_spmd} | conditional | flops 100767752 | bytes 12947604 | solution.py:74
  343.7 8.2 %conditional.2 = (f32[96,1024]{1,0:T(8,128)S(1)}) conditional(s32[]{:T(128)} %convert_element_type.9, f32[96,1024]{1,0:T(8,128)S(1)} %get-tuple-element.393, (s32[]{:T(128)}, bf16[96,32768]{1,0:T(8,128)(2,1)}, s32[]{:T(128)}, bf16[65536]{0:T(1024)(128)(2,1)}, f32[96,1024]{1,0:T(8,128)S(1)}) %tuple.80), branch_computations={%region_5.5_spmd, %region_6.6_spmd} | conditional | flops 100767752 | bytes 12947604 | solution.py:74
  360.2 8.2 %conditional.2 = (f32[96,1024]{1,0:T(8,128)S(1)}) conditional(s32[]{:T(128)} %convert_element_type.9, f32[96,1024]{1,0:T(8,128)S(1)} %get-tuple-element.393, (s32[]{:T(128)}, bf16[96,32768]{1,0:T(8,128)(2,1)}, s32[]{:T(128)}, bf16[65536]{0:T(1024)(128)(2,1)}, f32[96,1024]{1,0:T(8,128)S(1)}) %tuple.80), branch_computations={%region_5.5_spmd, %region_6.6_spmd} | conditional | flops 100767752 | bytes 12947604 | solution.py:74
  368.5 8.2 %conditional.2 = (f32[96,1024]{1,0:T(8,128)S(1)}) conditional(s32[]{:T(128)} %convert_element_type.9, f32[96,1024]{1,0:T(8,128)S(1)} %get-tuple-element.393, (s32[]{:T(128)}, bf16[96,32768]{1,0:T(8,128)(2,1)}, s32[]{:T(128)}, bf16[65536]{0:T(1024)(128)(2,1)}, f32[96,1024]{1,0:T(8,128)S(1)}) %tuple.80), branch_computations={%region_5.5_spmd, %region_6.6_spmd} | conditional | flops 100767752 | bytes 12947604 | solution.py:74
  376.8 8.2 %conditional.2 = (f32[96,1024]{1,0:T(8,128)S(1)}) conditional(s32[]{:T(128)} %convert_element_type.9, f32[96,1024]{1,0:T(8,128)S(1)} %get-tuple-element.393, (s32[]{:T(128)}, bf16[96,32768]{1,0:T(8,128)(2,1)}, s32[]{:T(128)}, bf16[65536]{0:T(1024)(128)(2,1)}, f32[96,1024]{1,0:T(8,128)S(1)}) %tuple.80), branch_computations={%region_5.5_spmd, %region_6.6_spmd} | conditional | flops 100767752 | bytes 12947604 | solution.py:74
  393.4 8.2 %conditional.2 = (f32[96,1024]{1,0:T(8,128)S(1)}) conditional(s32[]{:T(128)} %convert_element_type.9, f32[96,1024]{1,0:T(8,128)S(1)} %get-tuple-element.393, (s32[]{:T(128)}, bf16[96,32768]{1,0:T(8,128)(2,1)}, s32[]{:T(128)}, bf16[65536]{0:T(1024)(128)(2,1)}, f32[96,1024]{1,0:T(8,128)S(1)}) %tuple.80), branch_computations={%region_5.5_spmd, %region_6.6_spmd} | conditional | flops 100767752 | bytes 12947604 | solution.py:74
  401.6 8.2 %conditional.2 = (f32[96,1024]{1,0:T(8,128)S(1)}) conditional(s32[]{:T(128)} %convert_element_type.9, f32[96,1024]{1,0:T(8,128)S(1)} %get-tuple-element.393, (s32[]{:T(128)}, bf16[96,32768]{1,0:T(8,128)(2,1)}, s32[]{:T(128)}, bf16[65536]{0:T(1024)(128)(2,1)}, f32[96,1024]{1,0:T(8,128)S(1)}) %tuple.80), branch_computations={%region_5.5_spmd, %region_6.6_spmd} | conditional | flops 100767752 | bytes 12947604 | solution.py:74
  (618 shorter events, 895.7 us)
Async XLA Ops:
  7.2 187.5 %all-gather.4.cloned.1.call-start = ((), (), s32[]{:S(2)}) async-start(), calls=%async_computation | async-start | bytes 6488064 | tf_op jit(solution)/shard_map/all_gather | solution.py:56
  36.0 0.8 copy-start.2
  36.2 156.9 %copy-start = (bf16[32768]{0:T(1024)(128)(2,1)S(1)}, bf16[32768]{0:T(1024)(128)(2,1)}, u32[]{:S(2)}) copy-start(bf16[32768]{0:T(1024)(128)(2,1)} %param.13) | copy-start | bytes 196612
  194.7 529.8 %copy-start.1 = (f32[96]{0:T(128)S(1)}, f32[96]{0:T(128)}, u32[]{:S(2)}) copy-start(f32[96]{0:T(128)} %param.12) | copy-start | bytes 1156
Sparse Core Ops, SparseCore 0:
  10.6 83.9 all-gather.3
where the time goes:
time: 738 us; the launch traced here: 732 us
  local copies, waits for them, and re-layouts  450 us (61%)
  blocking collectives  152 us (21%)
  matrix products  77.3 us (10%)
  other arithmetic  30.8 us (4%)
  between operations  14.8 us (2%)
    another operation x128, local copies, waits for them, and re-layouts, toeplitz(): repeated = jnp.tile(pattern, rows_count)[:rows_count * (period - 1)]  173 us
    reshape x64, local copies, waits for them, and re-layouts, toeplitz(): return repeated.reshape(rows_count, period - 1)[:, :cols_count]  169 us
    unnamed x1, blocking collectives  111 us
    dot_general x64, matrix products, product(): return jnp.dot(source_block, matrix, preferred_element_type=jnp.float32)  77.3 us
    dynamic_slice x64, local copies, waits for them, and re-layouts, toeplitz(): lax.dynamic_slice_in_dim(padded, zero_pad + first_offset, cols_count)  49.2 us
    dynamic_slice x64, local copies, waits for them, and re-layouts, toeplitz(): lax.dynamic_slice_in_dim(padded, zero_pad + first_offset - (rows_count -...  48.7 us
    all_gather x1, blocking collectives, shards(): lax.all_gather(jnp.sum(counts, axis=0, dtype=jnp.int32)[None, :], 'cell',...  41.4 us
    another operation x3, other arithmetic  27.2 us
  transfers between devices with their start and end apart: 1, of which 0 were waited for; matrix products, arithmetic and copies ran while one was open for 4% of the time, Pallas kernels for 0%

commit v1 on v0

v1 whole, which is shorter than its diff:
```python
import jax
import jax.numpy as jnp
from jax import lax
from jax.experimental import pallas as pl
from jax.experimental.pallas import tpu as pltpu
from jax.sharding import PartitionSpec as P

SPANS = 32
CELLS = 96
STEPS = 1024
BLK = 256
ROWS = 16
TILES = 256

VMEM = pl.BlockSpec(memory_space=pltpu.VMEM)
ANY = pl.BlockSpec(memory_space=pl.ANY)


def pack_kernel(noise_ref, inc_ref, out_ref, scr):
    x = noise_ref[...].astype(jnp.float32)
    for c in range(3):
        for g in range(4):
            for k in range(4):
                for h in range(2):
                    col = 256 * k + 128 * h
                    tile = x[32 * c + 8 * g:32 * c + 8 * g + 8, col:col + 128]
                    scr[h, pl.ds(8 * g * ROWS + 3 * k + c, 8, stride=ROWS), :] = tile
    inc = inc_ref[...].astype(jnp.float32).astype(jnp.bfloat16)
    inc = jnp.concatenate([inc, jnp.zeros((32, STEPS), jnp.bfloat16)], axis=0)
    ones = jnp.ones((8, STEPS), jnp.bfloat16)
    sums = lax.dot_general(ones, inc, (((1,), (1,)), ((), ())), preferred_element_type=jnp.float32)
    high = jnp.floor(sums * (1.0 / 64.0))
    low = sums - 64.0 * high
    zero = jnp.zeros((8, 128), jnp.float32)
    for g in range(4):
        for r, v in ((12, high), (13, low), (14, zero), (15, zero)):
            scr[0, pl.ds(8 * g * ROWS + r, 8, stride=ROWS), :] = v
            scr[1, pl.ds(8 * g * ROWS + r, 8, stride=ROWS), :] = zero
    for h in range(2):
        out_ref[:, :, 128 * h:128 * h + 128] = scr[h].astype(jnp.bfloat16).reshape(SPANS, ROWS, 128)


def table_kernel(factor_ref, tab_ref):
    row = lax.broadcasted_iota(jnp.int32, (128, 128), 0)
    col = lax.broadcasted_iota(jnp.int32, (128, 128), 1)
    keep = col >= row
    tab_ref[0] = jnp.zeros((128, 128), jnp.bfloat16)

    def rolled(l):
        line = jnp.broadcast_to(factor_ref[pl.ds(l, 1), :], (128, 128))
        return pltpu.roll(line, 0, 1, stride=1, stride_axis=0)

    def step(l, before):
        now = rolled(l)
        tab_ref[l + 1] = jnp.where(keep, now, before).astype(jnp.bfloat16)
        return now

    lax.fori_loop(0, TILES, step, jnp.zeros((128, 128), jnp.float32), unroll=4)


def local_kernel(inc_ref, counts_ref, line_ref):
    inc = inc_ref[...].astype(jnp.float32).astype(jnp.bfloat16)
    row = lax.broadcasted_iota(jnp.int32, (BLK, BLK), 0)
    col = lax.broadcasted_iota(jnp.int32, (BLK, BLK), 1)
    tri = jnp.where(row <= col, 1.0, 0.0).astype(jnp.bfloat16)
    full = jnp.ones((BLK, BLK), jnp.bfloat16)
    for k in range(4):
        mat = jnp.concatenate([full] * k + [tri], axis=0)
        part = jnp.dot(inc[:, :BLK * (k + 1)], mat, preferred_element_type=jnp.float32)
        counts_ref[:, BLK * k:BLK * (k + 1)] = part.astype(jnp.int32)
        total = jnp.sum(part, axis=0, keepdims=True)
        for h in range(2):
            line_ref[2 * k + h:2 * k + h + 1, :] = total[:, 128 * h:128 * h + 128]


def conv_kernel(recv_ref, tab_hbm, mask_ref, line_ref, out_ref, carry_ref, group_ref, tab, xf, xs, acc, sems):
    def fetch(part):
        first = 64 * part + (part > 0)
        size = 64 + (part == 0)
        return pltpu.make_async_copy(tab_hbm.at[pl.ds(first, size)], tab.at[pl.ds(first, size)], sems.at[part])

    for part in range(4):
        fetch(part).start()

    flat = recv_ref[...].reshape(SPANS * ROWS, BLK)
    xs[:, 0:BLK] = flat
    within = lax.broadcasted_iota(jnp.int32, (512, 128), 0) % ROWS
    for h in range(2):
        xf[h, 0:16, :] = jnp.zeros((16, 128), jnp.float32)
        xf[h, 16:528, :] = flat[:, 128 * h:128 * h + 128].astype(jnp.float32)
        for e in range(1, 4):
            same = xf[h, 16 - 3 * e:528 - 3 * e, :]
            prev = xf[h, 12 - 3 * e:524 - 3 * e, :]
            lane = BLK * e + 128 * h
            xs[:, lane:lane + 128] = jnp.where(within >= 3 * e, same, prev).astype(jnp.bfloat16)

    high = xf[0, pl.ds(28, SPANS, stride=ROWS), :].astype(jnp.bfloat16)
    low = xf[0, pl.ds(29, SPANS, stride=ROWS), :].astype(jnp.bfloat16)
    mask = mask_ref[...]
    dims = (((0,), (0,)), ((), ()))
    carried = 64.0 * lax.dot_general(high, mask, dims, preferred_element_type=jnp.float32)
    carried = (carried + lax.dot_general(low, mask, dims, preferred_element_type=jnp.float32))[:CELLS]
    carry_ref[...] = carried.astype(jnp.int32)
    group = (line_ref[...] + jnp.sum(carried, axis=0, keepdims=True)).astype(jnp.int32)
    for d in range(8):
        group_ref[d] = group

    acc[...] = jnp.zeros_like(acc)
    for grp in range(4):
        fetch(grp).wait()
        rows = 512 - 128 * grp

        def step(i, nothing, grp=grp, rows=rows):
            delta = 8 * grp + i
            parts = []
            for e in range(4):
                at = 2 * (4 * delta + e)
                t0, t1, t2 = tab[at], tab[at + 1], tab[at + 2]
                parts.append(jnp.concatenate([t1, t2], axis=1))
                parts.append(jnp.concatenate([t0, t1], axis=1))
            weights = jnp.concatenate(parts, axis=0)
            to = pl.ds(pl.multiple_of(ROWS * delta, ROWS), rows)
            acc[to, :] += jnp.dot(xs[0:rows, :], weights, preferred_element_type=jnp.float32)
            return nothing

        lax.fori_loop(0, 8, step, 0)

    for q in range(SPANS):
        base = ROWS * q
        for h in range(2):
            out_ref[q, 8 * h:8 * h + 8, :] = acc[base:base + 8, 128 * h:128 * h + 128]
            out_ref[q, 16 + 4 * h:20 + 4 * h, :] = acc[base + 8:base + 12, 128 * h:128 * h + 128]


def counts_kernel(counts_ref, carry_ref, groups_ref, out_ref, total_ref):
    carry = carry_ref[...]
    for j in range(8):
        out_ref[:, 128 * j:128 * j + 128] = counts_ref[:, 128 * j:128 * j + 128] + carry
    total_ref[...] = jnp.sum(groups_ref[...], axis=0)


def spread_kernel(back_ref, scale_ref, out_ref):
    for c in range(3):
        for g in range(4):
            top = 32 * c + 8 * g
            scale = jnp.broadcast_to(scale_ref[top:top + 8, :], (8, 128))
            for k in range(4):
                r = 3 * k + c
                for h in range(2):
                    sub = 8 * h + r if r < 8 else 8 + 4 * h + r
                    tile = back_ref[pl.ds(192 * g + sub, 8, stride=24), :]
                    out_ref[top:top + 8, 256 * k + 128 * h:256 * k + 128 * h + 128] = tile * scale


def call(kernel, outs, args, in_specs=None, scratch=(), name=None, flops=0):
    return pl.pallas_call(
        kernel,
        out_shape=outs,
        in_specs=in_specs or [VMEM] * len(args),
        out_specs=jax.tree.map(lambda _: VMEM, outs),
        scratch_shapes=scratch,
        name=name,
        cost_estimate=pl.CostEstimate(flops=flops, transcendentals=0, bytes_accessed=1 << 20),
    )(*args)


def shards(increments, noise, noise_scale, factor):
    f32, i32, bf16 = jnp.float32, jnp.int32, jnp.bfloat16
    sds = jax.ShapeDtypeStruct
    position = lax.axis_index("tm")
    message = call(pack_kernel, sds((SPANS, ROWS, BLK), bf16), (noise, increments),
                   scratch=[pltpu.VMEM((2, SPANS * ROWS, 128), f32)], name="pack")
    received = lax.all_to_all(message, "tm", 0, 0, tiled=True)
    table = call(table_kernel, sds((TILES + 1, 128, 128), bf16), (factor.reshape(TILES, 128).astype(f32),), name="table")
    local, line = call(local_kernel, (sds((CELLS, STEPS), i32), sds((8, 128), f32)), (increments,), name="local")
    mask = jnp.broadcast_to((jnp.arange(SPANS) < position)[:, None], (SPANS, 128)).astype(bf16)
    sent, carry, group = call(
        conv_kernel,
        (sds((SPANS, 24, 128), f32), sds((CELLS, 128), i32), sds((8, 8, 128), i32)),
        (received, table, mask, line),
        in_specs=[VMEM, ANY, VMEM, VMEM],
        scratch=[
            pltpu.VMEM((TILES + 1, 128, 128), bf16),
            pltpu.VMEM((2, 528, 128), f32),
            pltpu.VMEM((512, 4 * BLK), bf16),
            pltpu.VMEM((640, BLK), f32),
            pltpu.SemaphoreType.DMA((4,)),
        ],
        name="conv",
    )
    back = lax.all_to_all(sent, "tm", 0, 0, tiled=True)
    groups = lax.all_to_all(group, "cell", 0, 0, tiled=True)
    counts, total = call(counts_kernel, (sds((CELLS, STEPS), i32), sds((8, 128), i32)), (local, carry, groups), name="counts")
    correlated = call(spread_kernel, sds((CELLS, STEPS), f32), (back.reshape(SPANS * 24, 128), noise_scale[:, None]), name="spread")
    return counts, correlated, total.reshape(STEPS)


def solution(mesh):
    return jax.shard_map(
        shards,
        mesh=mesh,
        in_specs=(P("cell", "tm"), P("cell", "tm"), P("cell"), P()),
        out_specs=(P("cell", "tm"), P("cell", "tm"), P("tm")),
        check_vma=False,
    )
```

time: 738 us -> 82 us (0.11)
  the two profiles are of different devices: /device:TPU:249 before, /device:TPU:32 now
where the time goes in v1:
time: 82 us; the launch traced here: 81.5 us
  Pallas kernels  33.9 us (41%)
  starting transfers between devices  21.1 us (26%)
  waiting for transfers between devices  12.3 us (15%)
  blocking collectives  9.86 us (12%)
  local copies, waits for them, and re-layouts  2.16 us (3%)
  other arithmetic  1.5 us (2%)
    pallas_call x6, Pallas kernels, call(): pl.pallas_call(kernel, out_shape=outs, in_specs=in_specs or [VMEM] * len(...  33.9 us
    all_to_all x1, waiting for transfers between devices, shards(): back = lax.all_to_all(sent, 'tm', 0, 0, tiled=True)  12.3 us
    all_to_all x1, starting transfers between devices, shards(): received = lax.all_to_all(message, 'tm', 0, 0, tiled=True)  11.4 us
    all_to_all x1, blocking collectives, shards(): groups = lax.all_to_all(group, 'cell', 0, 0, tiled=True)  9.86 us
    all_to_all x1, starting transfers between devices, shards(): back = lax.all_to_all(sent, 'tm', 0, 0, tiled=True)  9.79 us
  transfers between devices with their start and end apart: 2, of which 1 were waited for; matrix products, arithmetic and copies ran while one was open for 3% of the time, Pallas kernels for 19%

profile of v1, /device:TPU:32, one launch (start us, length us, event | category | flops | bytes accessed | tf_op | source)
XLA Modules:
  0.0 81.5 jit_solution(3866223371476044645)
XLA Ops:
  0.6 2.0 %pack.1 = bf16[32,16,256]{2,1,0:T(8,128)(2,1)} custom-call(bf16[96,1024]{1,0:T(8,128)(2,1)} %noise_ref.1, s32[96,1024]{1,0:T(8,128)} %inc_ref.3), custom_call_target="tpu_custom_call" | custom-call | bytes 1048576 | tf_op jit(solution)/shard_map/pack/pallas_call | solution.py:156
  2.7 11.4 %all-to-all-start = ((bf16[32,16,256]{2,1,0:T(8,128)(2,1)}), bf16[32,16,256]{2,1,0:T(8,128)(2,1)S(1)}, u32[]{:S(2)}, u32[]{:S(2)}) async-start(bf16[32,16,256]{2,1,0:T(8,128)(2,1)} %pack.1), calls=%async_computation | async-start | bytes 524288 | tf_op jit(solution)/shard_map/all_to_all | solution.py:173
  14.0 2.0 %local.1 = (s32[96,1024]{1,0:T(8,128)}, f32[8,128]{1,0:T(8,128)}) custom-call(s32[96,1024]{1,0:T(8,128)} %inc_ref.3), custom_call_target="tpu_custom_call" | custom-call | bytes 1048576 | tf_op jit(solution)/shard_map/local/pallas_call | solution.py:156
  16.1 1.5 %bitcast_convert_fusion.factor_ref = f32[256,128]{1,0:T(8,128)} fusion(bf16[32768]{0:T(1024)(128)(2,1)} %param.7), kind=kLoop, calls=%fused_computation | loop fusion | flops 32768 | bytes 196608 | tf_op jit(solution)/shard_map/convert_element_type | solution.py:174
  17.6 0.0 copy-start.2
  17.6 11.8 %table.1.tab_hbm = bf16[257,128,128]{2,1,0:T(8,128)(2,1)} custom-call(f32[256,128]{1,0:T(8,128)} %bitcast_convert_fusion.factor_ref), custom_call_target="tpu_custom_call" | custom-call | bytes 1048576 | tf_op jit(solution)/shard_map/table/pallas_call | solution.py:156
  29.4 0.0 all-to-all-done.recv_ref
  29.4 0.0 copy-start.1
  29.4 0.7 broadcast_in_dim.4.mask_ref
  30.1 0.0 copy-done.1
  30.1 14.3 %conv.1 = (f32[32,24,128]{2,1,0:T(8,128)}, s32[96,128]{1,0:T(8,128)}, s32[8,8,128]{2,1,0:T(8,128)}) custom-call(bf16[32,16,256]{2,1,0:T(8,128)(2,1)} %copy-done.1, bf16[257,128,128]{2,1,0:T(8,128)(2,1)} %table.1.tab_hbm, bf16[32,128]{1,0:T(8,128)(2,1)} %broadcast_in_dim.4.mask_ref, f32[8,128]{1,0:T(8,128)} %get-tuple-element.11.line_ref), custom_call_target="tpu_custom_call" | custom-call | bytes 1048576 | tf_op jit(solution)/shard_map/conv/pallas_call | solution.py:156
  44.4 9.9 %all_to_all.15.groups_ref = s32[8,8,128]{2,1,0:T(8,128)} all-to-all(s32[8,8,128]{2,1,0:T(8,128)} %get-tuple-element.13), channel_id=1, replica_groups=mesh['tm'=32,'cell'=8] {'cell'}, dimensions={0} | all-to-all | bytes 65536 | tf_op jit(solution)/shard_map/all_to_all | solution.py:192
  54.3 9.8 %all-to-all-start.2 = ((f32[32,24,128]{2,1,0:T(8,128)}), f32[32,24,128]{2,1,0:T(8,128)S(1)}, u32[]{:S(2)}, u32[]{:S(2)}) async-start(f32[32,24,128]{2,1,0:T(8,128)} %get-tuple-element.15), calls=%async_computation.2 | async-start | bytes 786432 | tf_op jit(solution)/shard_map/all_to_all | solution.py:191
  64.1 0.0 copy-done.2
  64.1 0.7 copy.7.scale_ref
  64.8 1.8 %counts.1 = (s32[96,1024]{1,0:T(8,128)}, s32[8,128]{1,0:T(8,128)}) custom-call(s32[96,1024]{1,0:T(8,128)} %get-tuple-element.10.counts_ref, s32[96,128]{1,0:T(8,128)} %get-tuple-element.12.carry_ref, s32[8,8,128]{2,1,0:T(8,128)} %all_to_all.15.groups_ref), custom_call_target="tpu_custom_call" | custom-call | bytes 1048576 | tf_op jit(solution)/shard_map/counts/pallas_call | solution.py:156
  66.6 12.3 %all-to-all-done.2 = f32[32,24,128]{2,1,0:T(8,128)S(1)} async-done(((f32[32,24,128]{2,1,0:T(8,128)}), f32[32,24,128]{2,1,0:T(8,128)S(1)}, u32[]{:S(2)}, u32[]{:S(2)}) %all-to-all-start.2) | async-done | bytes 393248 | tf_op jit(solution)/shard_map/all_to_all | solution.py:191
  78.9 0.0 copy-start
  78.9 0.7 copy-done
  79.6 1.9 %spread.1 = f32[96,1024]{1,0:T(8,128)} custom-call(f32[768,128]{1,0:T(8,128)} %bitcast.6, f32[96,1]{1,0:T(8,128)} %copy.7.scale_ref), custom_call_target="tpu_custom_call" | custom-call | bytes 1048576 | tf_op jit(solution)/shard_map/spread/pallas_call | solution.py:156
  (1 shorter events, 0.0 us)
Async XLA Ops:
  2.7 26.7 %all-to-all-start = ((bf16[32,16,256]{2,1,0:T(8,128)(2,1)}), bf16[32,16,256]{2,1,0:T(8,128)(2,1)S(1)}, u32[]{:S(2)}, u32[]{:S(2)}) async-start(bf16[32,16,256]{2,1,0:T(8,128)(2,1)} %pack.1), calls=%async_computation | async-start | bytes 524288 | tf_op jit(solution)/shard_map/all_to_all | solution.py:173
  17.6 46.5 %copy-start.2 = (f32[96]{0:T(128)S(1)}, f32[96]{0:T(128)}, u32[]{:S(2)}) copy-start(f32[96]{0:T(128)} %param.6) | copy-start | bytes 1156
  29.4 0.7 copy-start.1
  54.3 24.6 %all-to-all-start.2 = ((f32[32,24,128]{2,1,0:T(8,128)}), f32[32,24,128]{2,1,0:T(8,128)S(1)}, u32[]{:S(2)}, u32[]{:S(2)}) async-start(f32[32,24,128]{2,1,0:T(8,128)} %get-tuple-element.15), calls=%async_computation.2 | async-start | bytes 786432 | tf_op jit(solution)/shard_map/all_to_all | solution.py:191
  78.9 0.7 copy-start

commit v2 on v0

v2 whole, which is shorter than its diff:
```python
import jax
import jax.numpy as jnp
from jax import lax
from jax.experimental import pallas as pl
from jax.experimental.pallas import tpu as pltpu
from jax.sharding import PartitionSpec as P

SPANS = 32
CELLS = 96
STEPS = 1024
BLK = 256
ROWS = 16
TILES = 256
FINE = 16
SHIFT = 3 * FINE
FAR = 128 // FINE
PART = TILES // FAR
SOON = 3

ON_CHIP = pl.BlockSpec(memory_space=pltpu.VMEM)
HBM = pl.BlockSpec(memory_space=pltpu.HBM)


def pack_kernel(noise_hbm, inc_hbm, out_hbm, x_ref, inc_ref, scr, out, sems):
    get_noise = pltpu.make_async_copy(noise_hbm, x_ref, sems.at[0])
    get_inc = pltpu.make_async_copy(inc_hbm, inc_ref, sems.at[1])
    get_inc.start()
    get_noise.start()
    get_inc.wait()
    inc = inc_ref[...].astype(jnp.float32).astype(jnp.bfloat16)
    inc = jnp.concatenate([inc, jnp.zeros((32, STEPS), jnp.bfloat16)], axis=0)
    ones = jnp.ones((8, STEPS), jnp.bfloat16)
    sums = lax.dot_general(ones, inc, (((1,), (1,)), ((), ())), preferred_element_type=jnp.float32)
    high = jnp.floor(sums * (1.0 / 64.0))
    low = sums - 64.0 * high
    zero = jnp.zeros((8, 128), jnp.float32)
    get_noise.wait()
    puts = []
    for g in range(4):
        base = 8 * g * ROWS
        for h in range(2):
            for c in range(3):
                top = 32 * c + 8 * g
                for k in range(4):
                    col = 256 * k + 128 * h
                    tile = x_ref[top:top + 8, col:col + 128].astype(jnp.float32)
                    scr[h, pl.ds(base + 3 * k + c, 8, stride=ROWS), :] = tile
            for r, v in ((12, high), (13, low), (14, zero), (15, zero)):
                scr[h, pl.ds(base + r, 8, stride=ROWS), :] = v if h == 0 else zero
            tile = scr[h, base:base + 8 * ROWS, :].astype(jnp.bfloat16)
            out[8 * g:8 * g + 8, :, 128 * h:128 * h + 128] = tile.reshape(8, ROWS, 128)
        some = pl.ds(8 * g, 8)
        puts.append(pltpu.make_async_copy(out.at[some], out_hbm.at[some], sems.at[2 + g]))
        puts[-1].start()
    for put in puts:
        put.wait()


def table_kernel(factor_ref, inc_hbm, tab_ref, counts_ref, line_ref, lines, inc_ref, sem):
    step = pl.program_id(0)
    first = step * PART
    get_inc = pltpu.make_async_copy(inc_hbm, inc_ref, sem.at[0])

    @pl.when(step == 0)
    def _():
        get_inc.start()
        lines[0:8, :] = jnp.zeros((8, 128), jnp.float32)
        lines[8:8 + TILES, :] = factor_ref[...].astype(jnp.float32)

    row = lax.broadcasted_iota(jnp.int32, (128, 128), 0)
    col = lax.broadcasted_iota(jnp.int32, (128, 128), 1)
    keep = col >= row

    def rolled(at):
        line = jnp.broadcast_to(lines[pl.ds(at, 1), :], (128, 128))
        return pltpu.roll(line, 0, 1, stride=1, stride_axis=0)

    before = rolled(first + 7)
    for i in range(PART):
        now = rolled(first + 8 + i)
        tab_ref[i] = jnp.where(keep, now, before).astype(jnp.bfloat16)
        before = now

    @pl.when(step == FAR - 1)
    def _():
        get_inc.wait()
        inc = inc_ref[...].astype(jnp.float32).astype(jnp.bfloat16)
        row = lax.broadcasted_iota(jnp.int32, (BLK, BLK), 0)
        col = lax.broadcasted_iota(jnp.int32, (BLK, BLK), 1)
        tri = jnp.where(row <= col, 1.0, 0.0).astype(jnp.bfloat16)
        full = jnp.ones((BLK, BLK), jnp.bfloat16)
        for k in range(4):
            mat = jnp.concatenate([full] * k + [tri], axis=0)
            part = jnp.dot(inc[:, :BLK * (k + 1)], mat, preferred_element_type=jnp.float32)
            counts_ref[:, BLK * k:BLK * (k + 1)] = part.astype(jnp.int32)
            total = jnp.sum(part, axis=0, keepdims=True)
            for h in range(2):
                line_ref[2 * k + h:2 * k + h + 1, :] = total[:, 128 * h:128 * h + 128]


def conv_kernel(recv_ref, tab_hbm, out_ref, tab, xf, xs, acc, sems):
    def fetch(part):
        lanes = pl.ds(PART * part, PART)
        return pltpu.make_async_copy(tab_hbm.at[lanes], tab.at[lanes], sems.at[part])

    for part in range(FAR):
        fetch(part).start()

    xf[:, 0:SHIFT, :] = jnp.zeros((2, SHIFT, 128), jnp.float32)
    for h in range(2):
        lanes = slice(128 * h, 128 * h + 128)
        for q in range(SPANS):
            xf[h, SHIFT + 12 * q:SHIFT + 12 * q + 12, :] = recv_ref[q, 0:12, lanes].astype(jnp.float32)
    for e in range(FINE):
        for h in range(2):
            lane = BLK * e + 128 * h
            xs[:, lane:lane + 128] = xf[h, SHIFT - 3 * e:SHIFT - 3 * e + 384, :].astype(jnp.bfloat16)

    for far in range(FAR):
        if far in (0, SOON):
            for part in range(far, SOON if far == 0 else FAR):
                fetch(part).wait()
        rows = 384 - SHIFT * far
        parts = []
        for e in range(FINE):
            at = 2 * (FINE * far + e)
            t0 = tab[at - 1] if at else jnp.zeros((128, 128), jnp.bfloat16)
            t1, t2 = tab[at], tab[at + 1]
            parts.append(jnp.concatenate([t1, t2], axis=1))
            parts.append(jnp.concatenate([t0, t1], axis=1))
        weights = jnp.concatenate(parts, axis=0)
        part = jnp.dot(xs[0:rows, :], weights, preferred_element_type=jnp.float32)
        if far == 0:
            acc[...] = part
        else:
            acc[SHIFT * far:, :] += part
        for q in range(4 * far, 4 * far + 4):
            for h in range(2):
                for r in range(0, 12, 4):
                    to = 8 * h + r if r < 8 else 16 + 4 * h
                    out_ref[q, to:to + 4, :] = acc[12 * q + r:12 * q + r + 4, 128 * h:128 * h + 128]


def carry_kernel(recv_ref, line_ref, carry_ref, group_ref):
    sums = recv_ref[:, 12:14, 0:128].astype(jnp.float32)
    high = sums[:, 0, :].astype(jnp.bfloat16)
    low = sums[:, 1, :].astype(jnp.bfloat16)
    span = lax.broadcasted_iota(jnp.int32, (SPANS, 128), 0)
    mask = jnp.where(span < lax.axis_index("tm"), 1.0, 0.0).astype(jnp.bfloat16)
    dims = (((0,), (0,)), ((), ()))
    carried = 64.0 * lax.dot_general(high, mask, dims, preferred_element_type=jnp.float32)
    carried = (carried + lax.dot_general(low, mask, dims, preferred_element_type=jnp.float32))[:CELLS]
    carry_ref[...] = carried.astype(jnp.int32)
    group_ref[...] = (line_ref[...] + jnp.sum(carried, axis=0, keepdims=True)).astype(jnp.int32)


def counts_kernel(counts_ref, carry_ref, a_ref, b_ref, c_ref, d_ref, out_ref, total_ref):
    carry = carry_ref[...]
    for j in range(8):
        out_ref[:, 128 * j:128 * j + 128] = counts_ref[:, 128 * j:128 * j + 128] + carry
    total_ref[...] = (a_ref[...] + b_ref[...]) + (c_ref[...] + d_ref[...])


def spread_kernel(back_ref, scale_ref, out_hbm, out, sems):
    copies = []
    for g in range(4):
        for c in range(3):
            top = 32 * c + 8 * g
            scale = jnp.broadcast_to(scale_ref[top:top + 8, :], (8, 128))
            for k in range(4):
                r = 3 * k + c
                for h in range(2):
                    sub = 8 * h + r if r < 8 else 8 + 4 * h + r
                    tile = back_ref[pl.ds(192 * g + sub, 8, stride=24), :]
                    out[top:top + 8, 256 * k + 128 * h:256 * k + 128 * h + 128] = tile * scale
            rows = pl.ds(top, 8)
            copies.append(pltpu.make_async_copy(out.at[rows], out_hbm.at[rows], sems.at[len(copies)]))
            copies[-1].start()
    for copy in copies:
        copy.wait()


def call(kernel, outs, args, in_specs=None, out_specs=None, scratch=(), **rest):
    return pl.pallas_call(
        kernel,
        out_shape=outs,
        in_specs=in_specs or [ON_CHIP] * len(args),
        out_specs=out_specs or jax.tree.map(lambda _: ON_CHIP, outs),
        scratch_shapes=scratch,
        compiler_params=pltpu.CompilerParams(vmem_limit_bytes=24 << 20),
        **rest,
    )(*args)


def on_chip(x):
    return pltpu.with_memory_space_constraint(x, pltpu.VMEM)


def in_hbm(x):
    return pltpu.with_memory_space_constraint(x, pltpu.HBM)


def steps(increments, noise, noise_scale, factor):
    f32, i32, bf16 = jnp.float32, jnp.int32, jnp.bfloat16
    sds = jax.ShapeDtypeStruct
    dma = pltpu.SemaphoreType.DMA
    message = call(
        pack_kernel, sds((SPANS, ROWS, BLK), bf16), (in_hbm(noise), in_hbm(increments)),
        in_specs=[HBM, HBM], out_specs=HBM,
        scratch=[pltpu.VMEM((CELLS, STEPS), bf16), pltpu.VMEM((CELLS, STEPS), i32),
                 pltpu.VMEM((2, SPANS * ROWS, 128), f32), pltpu.VMEM((SPANS, ROWS, BLK), bf16), dma((6,))],
    )
    received = lax.all_to_all(message, "tm", 0, 0, tiled=True)
    whole = lambda i: (0, 0)
    table, local, line = call(
        table_kernel,
        (pltpu.HBM((TILES, 128, 128), bf16), sds((CELLS, STEPS), i32), sds((8, 128), f32)),
        (in_hbm(factor.reshape(TILES, 128)), in_hbm(increments)),
        grid=(FAR,),
        in_specs=[pl.BlockSpec((TILES, 128), whole), HBM],
        out_specs=(pl.BlockSpec((PART, 128, 128), lambda i: (i, 0, 0)),
                   pl.BlockSpec((CELLS, STEPS), whole), pl.BlockSpec((8, 128), whole)),
        scratch=[pltpu.VMEM((8 + TILES, 128), f32), pltpu.VMEM((CELLS, STEPS), i32), dma((1,))],
    )
    sent = call(
        conv_kernel, sds((SPANS, 24, 128), f32), (on_chip(received), in_hbm(table)),
        in_specs=[ON_CHIP, HBM],
        scratch=[
            pltpu.VMEM((TILES, 128, 128), bf16),
            pltpu.VMEM((2, SHIFT + 384, 128), f32),
            pltpu.VMEM((384, FINE * BLK), bf16),
            pltpu.VMEM((384, BLK), f32),
            dma((FAR,)),
        ],
    )
    back = lax.all_to_all(sent, "tm", 0, 0, tiled=True)
    carry, group = call(carry_kernel, (sds((CELLS, 128), i32), sds((8, 128), i32)), (received, line))
    group = group + lax.ppermute(group, "cell", [(i, i ^ 1) for i in range(8)])
    others = [lax.ppermute(group, "cell", [(i, (i + 2 * k) % 8) for i in range(8)]) for k in (1, 2, 3)]
    counts, total = call(
        counts_kernel, (sds((CELLS, STEPS), i32), sds((8, 128), i32)), (local, carry, group, *others))
    correlated = call(
        spread_kernel, sds((CELLS, STEPS), f32), (on_chip(back.reshape(SPANS * 24, 128)), noise_scale[:, None]),
        out_specs=HBM, scratch=[pltpu.VMEM((CELLS, STEPS), f32), dma((12,))],
    )
    return counts, correlated, total.reshape(STEPS)


def solution(mesh):
    return jax.shard_map(
        steps,
        mesh=mesh,
        in_specs=(P("cell", "tm"), P("cell", "tm"), P("cell"), P()),
        out_specs=(P("cell", "tm"), P("cell", "tm"), P("tm")),
        check_vma=False,
    )
```

time: 738 us -> 56.9 us (0.08)
  the two profiles are of different devices: /device:TPU:249 before, /device:TPU:34 now
where the time goes in v2:
time: 56.9 us; the launch traced here: 56.6 us
  Pallas kernels  21.4 us (38%)
  starting transfers between devices  20.8 us (37%)
  waiting for transfers between devices  13.7 us (24%)
  between operations  0.69 us (1%)
    pallas_call x6, Pallas kernels, call(): pl.pallas_call(kernel, out_shape=outs, in_specs=in_specs or [ON_CHIP] * l...  21.4 us
    all_to_all x1, starting transfers between devices, steps(): received = lax.all_to_all(message, 'tm', 0, 0, tiled=True)  11.4 us
    all_to_all x1, waiting for transfers between devices, steps(): back = lax.all_to_all(sent, 'tm', 0, 0, tiled=True)  5.51 us
    all_to_all x1, waiting for transfers between devices, steps(): received = lax.all_to_all(message, 'tm', 0, 0, tiled=True)  5.26 us
    ppermute x3, starting transfers between devices, steps(): lax.ppermute(group, 'cell', [(i, (i + 2 * k) % 8) for i in range(8)])  4.76 us
    all_to_all x1, starting transfers between devices, steps(): back = lax.all_to_all(sent, 'tm', 0, 0, tiled=True)  4.59 us
    ppermute x3, waiting for transfers between devices, steps(): lax.ppermute(group, 'cell', [(i, (i + 2 * k) % 8) for i in range(8)])  1.74 us
    ppermute x1, waiting for transfers between devices, steps(): group = group + lax.ppermute(group, 'cell', [(i, i ^ 1) for i in range(8)])  1.15 us
  transfers between devices with their start and end apart: 6, of which 4 were waited for; matrix products, arithmetic and copies ran while one was open for 0% of the time, Pallas kernels for 14%

profile of v2, /device:TPU:34, one launch (start us, length us, event | category | flops | bytes accessed | tf_op | source)
XLA Modules:
  0.0 56.6 jit_solution(17299946822206275172)
XLA Ops:
  0.6 0.0 copy-start
  0.6 2.0 %shard_map.68 = bf16[32,16,256]{2,1,0:T(8,128)(2,1)} custom-call(bf16[96,1024]{1,0:T(8,128)(2,1)} %noise_hbm.1, s32[96,1024]{1,0:T(8,128)} %inc_hbm.3), custom_call_target="tpu_custom_call" | custom-call | tf_op jit(solution)/shard_map/pallas_call | solution.py:184
  2.7 11.4 %all-to-all-start = ((bf16[32,16,256]{2,1,0:T(8,128)(2,1)}), bf16[32,16,256]{2,1,0:T(8,128)(2,1)S(1)}, u32[]{:S(2)}, u32[]{:S(2)}) async-start(bf16[32,16,256]{2,1,0:T(8,128)(2,1)} %shard_map.68), calls=%async_computation | async-start | bytes 524288 | tf_op jit(solution)/shard_map/all_to_all | solution.py:213
  14.1 7.0 %shard_map.67 = (bf16[256,128,128]{2,1,0:T(8,128)(2,1)}, s32[96,1024]{1,0:T(8,128)S(1)}, f32[8,128]{1,0:T(8,128)S(1)}) custom-call(bf16[256,128]{1,0:T(8,128)(2,1)} %bitcast.5, s32[96,1024]{1,0:T(8,128)} %inc_hbm.3), custom_call_target="tpu_custom_call" | custom-call | tf_op jit(solution)/shard_map/pallas_call | solution.py:184
  21.1 5.3 %all-to-all-done.recv_ref = bf16[32,16,256]{2,1,0:T(8,128)(2,1)S(1)} async-done(((bf16[32,16,256]{2,1,0:T(8,128)(2,1)}), bf16[32,16,256]{2,1,0:T(8,128)(2,1)S(1)}, u32[]{:S(2)}, u32[]{:S(2)}) %all-to-all-start) | async-done | bytes 262176 | tf_op jit(solution)/shard_map/all_to_all | solution.py:213
  26.3 10.4 %shard_map.71 = f32[32,24,128]{2,1,0:T(8,128)} custom-call(bf16[32,16,256]{2,1,0:T(8,128)(2,1)S(1)} %all-to-all-done.recv_ref, bf16[256,128,128]{2,1,0:T(8,128)(2,1)} %get-tuple-element.15.tab_hbm), custom_call_target="tpu_custom_call" | custom-call | tf_op jit(solution)/shard_map/pallas_call | solution.py:184
  36.7 4.6 %all-to-all-start.1 = ((f32[32,24,128]{2,1,0:T(8,128)}), f32[32,24,128]{2,1,0:T(8,128)S(1)}, u32[]{:S(2)}, u32[]{:S(2)}) async-start(f32[32,24,128]{2,1,0:T(8,128)} %shard_map.71), calls=%async_computation.1 | async-start | bytes 786432 | tf_op jit(solution)/shard_map/all_to_all | solution.py:236
  41.3 0.2 shard_map.69
  41.6 0.1 collective-permute-start
  41.6 1.2 %collective-permute-done = s32[8,128]{1,0:T(8,128)S(1)} collective-permute-done((s32[8,128]{1,0:T(8,128)S(1)}, s32[8,128]{1,0:T(8,128)S(1)}, u32[]{:S(2)}, u32[]{:S(2)}) %collective-permute-start) | collective-permute-done | bytes 4128 | tf_op jit(solution)/shard_map/ppermute | solution.py:238
  42.8 1.5 %collective-permute-start.1 = (s32[8,128]{1,0:T(8,128)S(1)}, s32[8,128]{1,0:T(8,128)S(1)}, u32[]{:S(2)}, u32[]{:S(2)}) collective-permute-start(s32[8,128]{1,0:T(8,128)S(1)} %add.3.a_ref), channel_id=1, source_target_pairs={{0,2},{1,3},{2,4},{3,5},{4,6},{5,7},{6,0},{7,1},{8,10},{9,11},{10,... | collective-permute-start | bytes 12296 | tf_op jit(solution)/shard_map/ppermute | solution.py:239
  44.3 1.1 %collective-permute-start.2 = (s32[8,128]{1,0:T(8,128)S(1)}, s32[8,128]{1,0:T(8,128)S(1)}, u32[]{:S(2)}, u32[]{:S(2)}) collective-permute-start(s32[8,128]{1,0:T(8,128)S(1)} %add.3.a_ref), channel_id=1, source_target_pairs={{0,4},{1,5},{2,6},{3,7},{4,0},{5,1},{6,2},{7,3},{8,12},{9,13},{10,... | collective-permute-start | bytes 12296 | tf_op jit(solution)/shard_map/ppermute | solution.py:239
  45.4 2.2 %collective-permute-start.3 = (s32[8,128]{1,0:T(8,128)S(1)}, s32[8,128]{1,0:T(8,128)S(1)}, u32[]{:S(2)}, u32[]{:S(2)}) collective-permute-start(s32[8,128]{1,0:T(8,128)S(1)} %add.3.a_ref), channel_id=1, source_target_pairs={{0,6},{1,7},{2,0},{3,1},{4,2},{5,3},{6,4},{7,5},{8,14},{9,15},{10,... | collective-permute-start | bytes 12296 | tf_op jit(solution)/shard_map/ppermute | solution.py:239
  47.6 0.0 copy-done
  47.6 0.1 copy.7.scale_ref
  47.7 0.0 collective-permute-done.1.b_ref
  47.7 1.7 %collective-permute-done.2.c_ref = s32[8,128]{1,0:T(8,128)S(1)} collective-permute-done((s32[8,128]{1,0:T(8,128)S(1)}, s32[8,128]{1,0:T(8,128)S(1)}, u32[]{:S(2)}, u32[]{:S(2)}) %collective-permute-start.2) | collective-permute-done | bytes 4128 | tf_op jit(solution)/shard_map/ppermute | solution.py:239
  49.4 0.0 collective-permute-done.3.d_ref
  49.4 0.8 %shard_map.70 = (s32[96,1024]{1,0:T(8,128)}, s32[8,128]{1,0:T(8,128)}) custom-call(s32[96,1024]{1,0:T(8,128)S(1)} %get-tuple-element.10.counts_ref, s32[96,128]{1,0:T(8,128)S(1)} %get-tuple-element.12.carry_ref, s32[8,128]{1,0:T(8,128)S(1)} %add.3.a_ref, s32[8,128]{1,0:T(8,128)S(1)} %collective-permute-done.1.b_ref, ...), custom_call_target="tpu_custom_call" | custom-call | tf_op jit(solution)/shard_map/pallas_call | solution.py:184
  50.2 5.5 %all-to-all-done.1 = f32[32,24,128]{2,1,0:T(8,128)S(1)} async-done(((f32[32,24,128]{2,1,0:T(8,128)}), f32[32,24,128]{2,1,0:T(8,128)S(1)}, u32[]{:S(2)}, u32[]{:S(2)}) %all-to-all-start.1) | async-done | bytes 393248 | tf_op jit(solution)/shard_map/all_to_all | solution.py:236
  55.7 0.9 %shard_map.72 = f32[96,1024]{1,0:T(8,128)} custom-call(f32[768,128]{1,0:T(8,128)S(1)} %bitcast.4, f32[96,1]{1,0:T(8,128)S(1)} %copy.7.scale_ref), custom_call_target="tpu_custom_call" | custom-call | tf_op jit(solution)/shard_map/pallas_call | solution.py:184
  (1 shorter events, 0.0 us)
Async XLA Ops:
  0.6 46.9 %copy-start = (f32[96]{0:T(128)S(1)}, f32[96]{0:T(128)}, u32[]{:S(2)}) copy-start(f32[96]{0:T(128)} %param.6) | copy-start | bytes 1156
  2.7 23.6 %all-to-all-start = ((bf16[32,16,256]{2,1,0:T(8,128)(2,1)}), bf16[32,16,256]{2,1,0:T(8,128)(2,1)S(1)}, u32[]{:S(2)}, u32[]{:S(2)}) async-start(bf16[32,16,256]{2,1,0:T(8,128)(2,1)} %shard_map.68), calls=%async_computation | async-start | bytes 524288 | tf_op jit(solution)/shard_map/all_to_all | solution.py:213
  36.7 19.0 %all-to-all-start.1 = ((f32[32,24,128]{2,1,0:T(8,128)}), f32[32,24,128]{2,1,0:T(8,128)S(1)}, u32[]{:S(2)}, u32[]{:S(2)}) async-start(f32[32,24,128]{2,1,0:T(8,128)} %shard_map.71), calls=%async_computation.1 | async-start | bytes 786432 | tf_op jit(solution)/shard_map/all_to_all | solution.py:236
  41.6 1.2 %collective-permute-start = (s32[8,128]{1,0:T(8,128)S(1)}, s32[8,128]{1,0:T(8,128)S(1)}, u32[]{:S(2)}, u32[]{:S(2)}) collective-permute-start(s32[8,128]{1,0:T(8,128)S(1)} %get-tuple-element.13), channel_id=1, source_target_pairs={{0,1},{1,0},{2,3},{3,2},{4,5},{5,4},{6,7},{7,6},{8,9},{9,8},{10,11... | collective-permute-start | bytes 12296 | tf_op jit(solution)/shard_map/ppermute | solution.py:238
  42.8 4.9 %collective-permute-start.1 = (s32[8,128]{1,0:T(8,128)S(1)}, s32[8,128]{1,0:T(8,128)S(1)}, u32[]{:S(2)}, u32[]{:S(2)}) collective-permute-start(s32[8,128]{1,0:T(8,128)S(1)} %add.3.a_ref), channel_id=1, source_target_pairs={{0,2},{1,3},{2,4},{3,5},{4,6},{5,7},{6,0},{7,1},{8,10},{9,11},{10,... | collective-permute-start | bytes 12296 | tf_op jit(solution)/shard_map/ppermute | solution.py:239
  44.3 5.1 %collective-permute-start.2 = (s32[8,128]{1,0:T(8,128)S(1)}, s32[8,128]{1,0:T(8,128)S(1)}, u32[]{:S(2)}, u32[]{:S(2)}) collective-permute-start(s32[8,128]{1,0:T(8,128)S(1)} %add.3.a_ref), channel_id=1, source_target_pairs={{0,4},{1,5},{2,6},{3,7},{4,0},{5,1},{6,2},{7,3},{8,12},{9,13},{10,... | collective-permute-start | bytes 12296 | tf_op jit(solution)/shard_map/ppermute | solution.py:239
  45.4 4.0 %collective-permute-start.3 = (s32[8,128]{1,0:T(8,128)S(1)}, s32[8,128]{1,0:T(8,128)S(1)}, u32[]{:S(2)}, u32[]{:S(2)}) collective-permute-start(s32[8,128]{1,0:T(8,128)S(1)} %add.3.a_ref), channel_id=1, source_target_pairs={{0,6},{1,7},{2,0},{3,1},{4,2},{5,3},{6,4},{7,5},{8,14},{9,15},{10,... | collective-permute-start | bytes 12296 | tf_op jit(solution)/shard_map/ppermute | solution.py:239

commit v3 on v2

v3 whole, which is shorter than its diff:
```python
import jax
import jax.numpy as jnp
from jax import lax
from jax.experimental import pallas as pl
from jax.experimental.pallas import tpu as pltpu
from jax.sharding import PartitionSpec as P

SPANS = 32
CELLS = 96
STEPS = 1024
BLK = 256
ROWS = 16
TILES = 256
FINE = 16
SHIFT = 3 * FINE
STRIDE = 5
ORDER = [STRIDE * p % SPANS for p in range(SPANS)]
PLACE = [ORDER.index(q) for q in range(SPANS)]
FAR = 128 // FINE

ON_CHIP = pl.BlockSpec(memory_space=pltpu.VMEM)
HBM = pl.BlockSpec(memory_space=pltpu.HBM)


def pack_kernel(noise_hbm, inc_hbm, factor_hbm, out, strip_ref, x_ref, inc_ref, factor_ref, lines, scr, sems):
    get_noise = pltpu.make_async_copy(noise_hbm, x_ref, sems.at[0])
    get_inc = pltpu.make_async_copy(inc_hbm, inc_ref, sems.at[1])
    get_factor = pltpu.make_async_copy(factor_hbm, factor_ref, sems.at[2])
    get_factor.start()
    get_inc.start()
    get_noise.start()

    get_factor.wait()
    lines[...] = factor_ref[...].astype(jnp.float32)
    row = lax.broadcasted_iota(jnp.int32, (16, 128), 0)
    col = lax.broadcasted_iota(jnp.int32, (16, 128), 1)
    keep = col >= row
    before = jnp.zeros((16, 128), jnp.float32)
    for tile in range(TILES):
        line = jnp.broadcast_to(lines[tile:tile + 1, :], (16, 128))
        now = pltpu.roll(line, 0, 1, stride=1, stride_axis=0)
        strip_ref[tile] = jnp.where(keep, now, before).astype(jnp.bfloat16)
        before = now

    get_inc.wait()
    inc = inc_ref[...].astype(jnp.float32).astype(jnp.bfloat16)
    inc = jnp.concatenate([inc, jnp.zeros((32, STEPS), jnp.bfloat16)], axis=0)
    ones = jnp.ones((8, STEPS), jnp.bfloat16)
    sums = lax.dot_general(ones, inc, (((1,), (1,)), ((), ())), preferred_element_type=jnp.float32)
    high = jnp.floor(sums * (1.0 / 64.0))
    low = sums - 64.0 * high
    zero = jnp.zeros((8, 128), jnp.float32)
    get_noise.wait()
    for g in range(4):
        base = 8 * g * ROWS
        for h in range(2):
            for c in range(3):
                top = 32 * c + 8 * g
                for k in range(4):
                    col = 256 * k + 128 * h
                    tile = x_ref[top:top + 8, col:col + 128].astype(jnp.float32)
                    scr[h, pl.ds(base + 3 * k + c, 8, stride=ROWS), :] = tile
            for r, v in ((12, high), (13, low), (14, zero), (15, zero)):
                scr[h, pl.ds(base + r, 8, stride=ROWS), :] = v if h == 0 else zero
            tile = scr[h, base:base + 8 * ROWS, :].astype(jnp.bfloat16)
            out[8 * g:8 * g + 8, :, 128 * h:128 * h + 128] = tile.reshape(8, ROWS, 128)


def local_kernel(inc_hbm, counts_ref, line_ref, inc_ref, sem):
    get_inc = pltpu.make_async_copy(inc_hbm, inc_ref, sem.at[0])
    get_inc.start()
    row = lax.broadcasted_iota(jnp.int32, (BLK, BLK), 0)
    col = lax.broadcasted_iota(jnp.int32, (BLK, BLK), 1)
    tri = jnp.where(row <= col, 1.0, 0.0).astype(jnp.bfloat16)
    full = jnp.ones((BLK, BLK), jnp.bfloat16)
    get_inc.wait()
    inc = inc_ref[...].astype(jnp.float32).astype(jnp.bfloat16)
    for k in range(4):
        mat = jnp.concatenate([full] * k + [tri], axis=0)
        part = jnp.dot(inc[:, :BLK * (k + 1)], mat, preferred_element_type=jnp.float32)
        counts_ref[:, BLK * k:BLK * (k + 1)] = part.astype(jnp.int32)
        total = jnp.sum(part, axis=0, keepdims=True)
        for h in range(2):
            line_ref[2 * k + h:2 * k + h + 1, :] = total[:, 128 * h:128 * h + 128]


def conv_kernel(recv_ref, strip, out_ref, xf, xs, acc):
    xf[:, 0:SHIFT, :] = jnp.zeros((2, SHIFT, 128), jnp.float32)
    for h in range(2):
        lanes = slice(128 * h, 128 * h + 128)
        for q in range(SPANS):
            xf[h, SHIFT + 12 * q:SHIFT + 12 * q + 12, :] = recv_ref[PLACE[q], 0:12, lanes].astype(jnp.float32)
    for e in range(FINE):
        for h in range(2):
            lane = BLK * e + 128 * h
            xs[:, lane:lane + 128] = xf[h, SHIFT - 3 * e:SHIFT - 3 * e + 384, :].astype(jnp.bfloat16)

    col = lax.broadcasted_iota(jnp.int32, (16, 128), 1)
    zero = jnp.zeros((16, 128), jnp.bfloat16)

    def rolls(tile):
        if tile < 0:
            return [zero] * 8
        base = strip[tile]
        return [base] + [pltpu.roll(base, 16 * i, 1) for i in range(1, 8)]

    def square(now, before):
        return jnp.concatenate(
            [now[0]] + [jnp.where(col >= 16 * i, now[i], before[i]) for i in range(1, 8)], axis=0)

    for far in range(FAR):
        rows = 384 - SHIFT * far
        first = 2 * FINE * far
        rolled = {tile: rolls(tile) for tile in range(first - 2, first + 2 * FINE)}
        squares = {tile: square(rolled[tile], rolled[tile - 1]) for tile in range(first - 1, first + 2 * FINE)}
        parts = []
        for e in range(FINE):
            at = first + 2 * e
            parts.append(jnp.concatenate([squares[at], squares[at + 1]], axis=1))
            parts.append(jnp.concatenate([squares[at - 1], squares[at]], axis=1))
        weights = jnp.concatenate(parts, axis=0)
        part = jnp.dot(xs[0:rows, :], weights, preferred_element_type=jnp.float32)
        if far == 0:
            acc[...] = part
        else:
            acc[SHIFT * far:, :] += part
        for q in range(4 * far, 4 * far + 4):
            for h in range(2):
                for r in range(0, 12, 4):
                    to = 8 * h + r if r < 8 else 16 + 4 * h
                    out_ref[PLACE[q], to:to + 4, :] = acc[12 * q + r:12 * q + r + 4, 128 * h:128 * h + 128]


def carry_kernel(recv_ref, line_ref, carry_ref, group_ref):
    sums = recv_ref[:, 12:14, 0:128].astype(jnp.float32)
    high = sums[:, 0, :].astype(jnp.bfloat16)
    low = sums[:, 1, :].astype(jnp.bfloat16)
    span = STRIDE * lax.broadcasted_iota(jnp.int32, (SPANS, 128), 0) % SPANS
    mask = jnp.where(span < lax.axis_index("tm"), 1.0, 0.0).astype(jnp.bfloat16)
    dims = (((0,), (0,)), ((), ()))
    carried = 64.0 * lax.dot_general(high, mask, dims, preferred_element_type=jnp.float32)
    carried = (carried + lax.dot_general(low, mask, dims, preferred_element_type=jnp.float32))[:CELLS]
    carry_ref[...] = carried.astype(jnp.int32)
    group_ref[...] = (line_ref[...] + jnp.sum(carried, axis=0, keepdims=True)).astype(jnp.int32)


def counts_kernel(counts_ref, carry_ref, out_ref):
    carry = carry_ref[...]
    for j in range(8):
        out_ref[:, 128 * j:128 * j + 128] = counts_ref[:, 128 * j:128 * j + 128] + carry


def spread_kernel(back_ref, scale_ref, out_hbm, out, sems):
    copies = []
    for g in range(4):
        for c in range(3):
            top = 32 * c + 8 * g
            scale = jnp.broadcast_to(scale_ref[top:top + 8, :], (8, 128))
            for k in range(4):
                r = 3 * k + c
                for h in range(2):
                    sub = 8 * h + r if r < 8 else 8 + 4 * h + r
                    tile = back_ref[pl.ds(192 * g + sub, 8, stride=24), :]
                    out[top:top + 8, 256 * k + 128 * h:256 * k + 128 * h + 128] = tile * scale
            rows = pl.ds(top, 8)
            copies.append(pltpu.make_async_copy(out.at[rows], out_hbm.at[rows], sems.at[len(copies)]))
            copies[-1].start()
    for copy in copies:
        copy.wait()


def call(kernel, outs, args, in_specs=None, out_specs=None, scratch=(), **rest):
    return pl.pallas_call(
        kernel,
        out_shape=outs,
        in_specs=in_specs or [ON_CHIP] * len(args),
        out_specs=out_specs or jax.tree.map(lambda _: ON_CHIP, outs),
        scratch_shapes=scratch,
        compiler_params=pltpu.CompilerParams(vmem_limit_bytes=24 << 20),
        **rest,
    )(*args)


def on_chip(x):
    return pltpu.with_memory_space_constraint(x, pltpu.VMEM)


def in_hbm(x):
    return pltpu.with_memory_space_constraint(x, pltpu.HBM)


def steps(increments, noise, noise_scale, factor):
    f32, i32, bf16 = jnp.float32, jnp.int32, jnp.bfloat16
    sds = jax.ShapeDtypeStruct
    dma = pltpu.SemaphoreType.DMA
    chip = pltpu.VMEM
    message, strips = call(
        pack_kernel, (sds((SPANS, ROWS, BLK), bf16), chip((TILES, 16, 128), bf16)),
        (in_hbm(noise), in_hbm(increments), in_hbm(factor.reshape(TILES, 128))), in_specs=[HBM, HBM, HBM],
        scratch=[pltpu.VMEM((CELLS, STEPS), bf16), pltpu.VMEM((CELLS, STEPS), i32), pltpu.VMEM((TILES, 128), bf16),
                 pltpu.VMEM((TILES, 128), f32), pltpu.VMEM((2, SPANS * ROWS, 128), f32), dma((3,))],
    )
    received = lax.all_to_all(message, "tm", 0, 0, tiled=True, axis_index_groups=[ORDER])
    sent = call(
        conv_kernel, sds((SPANS, 24, 128), f32), (on_chip(received), on_chip(strips)),
        scratch=[
            pltpu.VMEM((2, SHIFT + 384, 128), f32),
            pltpu.VMEM((384, FINE * BLK), bf16),
            pltpu.VMEM((384, BLK), f32),
        ],
    )
    back = lax.all_to_all(sent, "tm", 0, 0, tiled=True, axis_index_groups=[ORDER])
    local, line = call(
        local_kernel, (sds((CELLS, STEPS), i32), sds((8, 128), f32)), (in_hbm(increments),), in_specs=[HBM],
        scratch=[pltpu.VMEM((CELLS, STEPS), i32), dma((1,))])
    carry, group = call(carry_kernel, (sds((CELLS, 128), i32), sds((8, 128), i32)), (received, line))
    group = group + lax.ppermute(group, "cell", [(i, i ^ 1) for i in range(8)])
    others = [lax.ppermute(group, "cell", [(i, (i + 2 * k) % 8) for i in range(8)]) for k in (1, 2, 3)]
    counts = call(counts_kernel, sds((CELLS, STEPS), i32), (local, carry))
    total = group + others[0] + others[1] + others[2]
    correlated = call(
        spread_kernel, sds((CELLS, STEPS), f32), (on_chip(back.reshape(SPANS * 24, 128)), noise_scale[:, None]),
        out_specs=HBM, scratch=[pltpu.VMEM((CELLS, STEPS), f32), dma((12,))],
    )
    return counts, correlated, total.reshape(STEPS)


def solution(mesh):
    return jax.shard_map(
        steps,
        mesh=mesh,
        in_specs=(P("cell", "tm"), P("cell", "tm"), P("cell"), P()),
        out_specs=(P("cell", "tm"), P("cell", "tm"), P("tm")),
        check_vma=False,
    )
```

time: 56.9 us -> 50.7 us (0.89)
  the two profiles are of different devices: /device:TPU:34 before, /device:TPU:36 now
where the time goes in v3:
time: 50.7 us; the launch traced here: 50.5 us
  blocking collectives  23.8 us (47%)
  Pallas kernels  9.78 us (19%)
  waiting for transfers between devices  7.94 us (16%)
  starting transfers between devices  7.57 us (15%)
  between operations  0.67 us (1%)
  other arithmetic  0.6 us (1%)
    all_to_all x1, blocking collectives, steps(): lax.all_to_all(message, 'tm', 0, 0, tiled=True, axis_index_groups=[ORDER])  23.8 us
    pallas_call x6, Pallas kernels, call(): pl.pallas_call(kernel, out_shape=outs, in_specs=in_specs or [ON_CHIP] * l...  9.78 us
    all_to_all x1, starting transfers between devices, steps(): lax.all_to_all(sent, 'tm', 0, 0, tiled=True, axis_index_groups=[ORDER])  4.22 us
    all_to_all x1, waiting for transfers between devices, steps(): lax.all_to_all(sent, 'tm', 0, 0, tiled=True, axis_index_groups=[ORDER])  4.07 us
    ppermute x3, starting transfers between devices, steps(): lax.ppermute(group, 'cell', [(i, (i + 2 * k) % 8) for i in range(8)])  3.27 us
    ppermute x3, waiting for transfers between devices, steps(): lax.ppermute(group, 'cell', [(i, (i + 2 * k) % 8) for i in range(8)])  2.71 us
    ppermute x1, waiting for transfers between devices, steps(): group = group + lax.ppermute(group, 'cell', [(i, i ^ 1) for i in range(8)])  1.15 us
  transfers between devices with their start and end apart: 5, of which 4 were waited for; matrix products, arithmetic and copies ran while one was open for 1% of the time, Pallas kernels for 5%

profile of v3, /device:TPU:36, one launch (start us, length us, event | category | flops | bytes accessed | tf_op | source)
XLA Modules:
  0.0 50.5 jit_solution(5976380943106240913)
XLA Ops:
  0.6 1.6 %shard_map.68 = (bf16[32,16,256]{2,1,0:T(8,128)(2,1)S(1)}, bf16[256,16,128]{2,1,0:T(8,128)(2,1)S(1)}) custom-call(bf16[96,1024]{1,0:T(8,128)(2,1)} %noise_hbm.1, s32[96,1024]{1,0:T(8,128)} %inc_hbm.3, bf16[256,128]{1,0:T(8,128)(2,1)} %bitcast.6), custom_call_target="tpu_custom_call" | custom-call | tf_op jit(solution)/shard_map/pallas_call | solution.py:173
  2.2 23.8 %all_to_all.10.recv_ref = bf16[32,16,256]{2,1,0:T(8,128)(2,1)S(1)} all-to-all(bf16[32,16,256]{2,1,0:T(8,128)(2,1)S(1)} %get-tuple-element.10), channel_id=1, replica_groups={{0,40,80,120,160,200,240,24,64,104,144,184,224,8,48,88,128,168,208,248,..., dimensions={0} | all-to-all | bytes 524288 | tf_op jit(solution)/shard_map/all_to_all | solution.py:203
  26.0 5.0 %shard_map.71 = f32[32,24,128]{2,1,0:T(8,128)} custom-call(bf16[32,16,256]{2,1,0:T(8,128)(2,1)S(1)} %all_to_all.10.recv_ref, bf16[256,16,128]{2,1,0:T(8,128)(2,1)S(1)} %get-tuple-element.13.strip), custom_call_target="tpu_custom_call" | custom-call | tf_op jit(solution)/shard_map/pallas_call | solution.py:173
  31.0 4.2 %all-to-all-start.1 = ((f32[32,24,128]{2,1,0:T(8,128)}), f32[32,24,128]{2,1,0:T(8,128)S(1)}, u32[]{:S(2)}, u32[]{:S(2)}) async-start(f32[32,24,128]{2,1,0:T(8,128)} %shard_map.71), calls=%async_computation.1 | async-start | bytes 786432 | tf_op jit(solution)/shard_map/all_to_all | solution.py:212
  35.2 1.3 %shard_map.67 = (s32[96,1024]{1,0:T(8,128)S(1)}, f32[8,128]{1,0:T(8,128)S(1)}) custom-call(s32[96,1024]{1,0:T(8,128)} %inc_hbm.3), custom_call_target="tpu_custom_call" | custom-call | tf_op jit(solution)/shard_map/pallas_call | solution.py:173
  36.5 0.2 shard_map.69
  36.7 0.1 collective-permute-start
  36.8 1.2 %collective-permute-done = s32[8,128]{1,0:T(8,128)S(1)} collective-permute-done((s32[8,128]{1,0:T(8,128)S(1)}, s32[8,128]{1,0:T(8,128)S(1)}, u32[]{:S(2)}, u32[]{:S(2)}) %collective-permute-start) | collective-permute-done | bytes 4128 | tf_op jit(solution)/shard_map/ppermute | solution.py:217
  38.0 0.0 copy-start
  38.0 0.5 %collective-permute-start.3 = (s32[8,128]{1,0:T(8,128)S(1)}, s32[8,128]{1,0:T(8,128)S(1)}, u32[]{:S(2)}, u32[]{:S(2)}) collective-permute-start(s32[8,128]{1,0:T(8,128)S(1)} %add.12), channel_id=1, source_target_pairs={{0,6},{1,7},{2,0},{3,1},{4,2},{5,3},{6,4},{7,5},{8,14},{9,15},{10,... | collective-permute-start | bytes 12296 | tf_op jit(solution)/shard_map/ppermute | solution.py:218
  38.5 2.7 %collective-permute-start.2 = (s32[8,128]{1,0:T(8,128)S(1)}, s32[8,128]{1,0:T(8,128)S(1)}, u32[]{:S(2)}, u32[]{:S(2)}) collective-permute-start(s32[8,128]{1,0:T(8,128)S(1)} %add.12), channel_id=1, source_target_pairs={{0,4},{1,5},{2,6},{3,7},{4,0},{5,1},{6,2},{7,3},{8,12},{9,13},{10,... | collective-permute-start | bytes 12296 | tf_op jit(solution)/shard_map/ppermute | solution.py:218
  41.3 0.0 collective-permute-start.1
  41.3 0.0 copy-done
  41.3 0.1 copy.7.scale_ref
  41.4 0.8 %shard_map.70 = s32[96,1024]{1,0:T(8,128)} custom-call(s32[96,1024]{1,0:T(8,128)S(1)} %get-tuple-element.9.counts_ref, s32[96,128]{1,0:T(8,128)S(1)} %get-tuple-element.12.carry_ref), custom_call_target="tpu_custom_call" | custom-call | tf_op jit(solution)/shard_map/pallas_call | solution.py:173
  42.1 0.0 collective-permute-done.3
  42.2 1.5 %collective-permute-done.2 = s32[8,128]{1,0:T(8,128)S(1)} collective-permute-done((s32[8,128]{1,0:T(8,128)S(1)}, s32[8,128]{1,0:T(8,128)S(1)}, u32[]{:S(2)}, u32[]{:S(2)}) %collective-permute-start.2) | collective-permute-done | bytes 4128 | tf_op jit(solution)/shard_map/ppermute | solution.py:218
  43.6 1.2 %collective-permute-done.1 = s32[8,128]{1,0:T(8,128)S(1)} collective-permute-done((s32[8,128]{1,0:T(8,128)S(1)}, s32[8,128]{1,0:T(8,128)S(1)}, u32[]{:S(2)}, u32[]{:S(2)}) %collective-permute-start.1) | collective-permute-done | bytes 4128 | tf_op jit(solution)/shard_map/ppermute | solution.py:218
  44.9 0.6 %add_bitcast_fusion = s32[1024]{0:T(1024)} fusion(s32[8,128]{1,0:T(8,128)S(1)} %collective-permute-done.3, s32[8,128]{1,0:T(8,128)S(1)} %collective-permute-done.2, s32[8,128]{1,0:T(8,128)S(1)} %add.12, s32[8,128]{1,0:T(8,128)S(1)} %collective-permute-done.1), kind=kLoop, calls=%fused_computation | loop fusion | flops 3072 | bytes 20480 | tf_op jit(solution)/shard_map/reshape | solution.py:225
  45.5 4.1 %all-to-all-done.1 = f32[32,24,128]{2,1,0:T(8,128)S(1)} async-done(((f32[32,24,128]{2,1,0:T(8,128)}), f32[32,24,128]{2,1,0:T(8,128)S(1)}, u32[]{:S(2)}, u32[]{:S(2)}) %all-to-all-start.1) | async-done | bytes 393248 | tf_op jit(solution)/shard_map/all_to_all | solution.py:212
  49.5 0.9 %shard_map.72 = f32[96,1024]{1,0:T(8,128)} custom-call(f32[768,128]{1,0:T(8,128)S(1)} %bitcast.5, f32[96,1]{1,0:T(8,128)S(1)} %copy.7.scale_ref), custom_call_target="tpu_custom_call" | custom-call | tf_op jit(solution)/shard_map/pallas_call | solution.py:173
  (1 shorter events, 0.0 us)
Async XLA Ops:
  31.0 18.6 %all-to-all-start.1 = ((f32[32,24,128]{2,1,0:T(8,128)}), f32[32,24,128]{2,1,0:T(8,128)S(1)}, u32[]{:S(2)}, u32[]{:S(2)}) async-start(f32[32,24,128]{2,1,0:T(8,128)} %shard_map.71), calls=%async_computation.1 | async-start | bytes 786432 | tf_op jit(solution)/shard_map/all_to_all | solution.py:212
  36.7 1.2 %collective-permute-start = (s32[8,128]{1,0:T(8,128)S(1)}, s32[8,128]{1,0:T(8,128)S(1)}, u32[]{:S(2)}, u32[]{:S(2)}) collective-permute-start(s32[8,128]{1,0:T(8,128)S(1)} %get-tuple-element.14), channel_id=1, source_target_pairs={{0,1},{1,0},{2,3},{3,2},{4,5},{5,4},{6,7},{7,6},{8,9},{9,8},{10,11... | collective-permute-start | bytes 12296 | tf_op jit(solution)/shard_map/ppermute | solution.py:217
  38.0 3.3 %copy-start = (f32[96]{0:T(128)S(1)}, f32[96]{0:T(128)}, u32[]{:S(2)}) copy-start(f32[96]{0:T(128)} %param.6) | copy-start | bytes 1156
  38.0 4.2 %collective-permute-start.3 = (s32[8,128]{1,0:T(8,128)S(1)}, s32[8,128]{1,0:T(8,128)S(1)}, u32[]{:S(2)}, u32[]{:S(2)}) collective-permute-start(s32[8,128]{1,0:T(8,128)S(1)} %add.12), channel_id=1, source_target_pairs={{0,6},{1,7},{2,0},{3,1},{4,2},{5,3},{6,4},{7,5},{8,14},{9,15},{10,... | collective-permute-start | bytes 12296 | tf_op jit(solution)/shard_map/ppermute | solution.py:218
  38.5 5.1 %collective-permute-start.2 = (s32[8,128]{1,0:T(8,128)S(1)}, s32[8,128]{1,0:T(8,128)S(1)}, u32[]{:S(2)}, u32[]{:S(2)}) collective-permute-start(s32[8,128]{1,0:T(8,128)S(1)} %add.12), channel_id=1, source_target_pairs={{0,4},{1,5},{2,6},{3,7},{4,0},{5,1},{6,2},{7,3},{8,12},{9,13},{10,... | collective-permute-start | bytes 12296 | tf_op jit(solution)/shard_map/ppermute | solution.py:218
  41.3 3.6 %collective-permute-start.1 = (s32[8,128]{1,0:T(8,128)S(1)}, s32[8,128]{1,0:T(8,128)S(1)}, u32[]{:S(2)}, u32[]{:S(2)}) collective-permute-start(s32[8,128]{1,0:T(8,128)S(1)} %add.12), channel_id=1, source_target_pairs={{0,2},{1,3},{2,4},{3,5},{4,6},{5,7},{6,0},{7,1},{8,10},{9,11},{10,... | collective-permute-start | bytes 12296 | tf_op jit(solution)/shard_map/ppermute | solution.py:218

commit v4 on v3

--- a/solution.py
+++ b/solution.py
@@ -1,3 +1,5 @@
+import math
+
 import jax
 import jax.numpy as jnp
 from jax import lax
@@ -13,8 +15,11 @@
 TILES = 256
 FINE = 16
 SHIFT = 3 * FINE
+LOG_TOP = math.log2(32000.0)
+TINY = 2.0 ** -100
 STRIDE = 5
-ORDER = [STRIDE * p % SPANS for p in range(SPANS)]
+FIRST = 31
+ORDER = [(STRIDE * p + FIRST) % SPANS for p in range(SPANS)]
 PLACE = [ORDER.index(q) for q in range(SPANS)]
 FAR = 128 // FINE
 
@@ -22,7 +27,7 @@
 HBM = pl.BlockSpec(memory_space=pltpu.HBM)
 
 
-def pack_kernel(noise_hbm, inc_hbm, factor_hbm, out, strip_ref, x_ref, inc_ref, factor_ref, lines, scr, sems):
+def pack_kernel(noise_hbm, inc_hbm, factor_hbm, out, strip_ref, small_ref, x_ref, inc_ref, factor_ref, lines, scr, sems):
     get_noise = pltpu.make_async_copy(noise_hbm, x_ref, sems.at[0])
     get_inc = pltpu.make_async_copy(inc_hbm, inc_ref, sems.at[1])
     get_factor = pltpu.make_async_copy(factor_hbm, factor_ref, sems.at[2])
@@ -44,6 +49,7 @@
 
     get_inc.wait()
     inc = inc_ref[...].astype(jnp.float32).astype(jnp.bfloat16)
+    small_ref[...] = inc
     inc = jnp.concatenate([inc, jnp.zeros((32, STEPS), jnp.bfloat16)], axis=0)
     ones = jnp.ones((8, STEPS), jnp.bfloat16)
     sums = lax.dot_general(ones, inc, (((1,), (1,)), ((), ())), preferred_element_type=jnp.float32)
@@ -66,15 +72,12 @@
             out[8 * g:8 * g + 8, :, 128 * h:128 * h + 128] = tile.reshape(8, ROWS, 128)
 
 
-def local_kernel(inc_hbm, counts_ref, line_ref, inc_ref, sem):
-    get_inc = pltpu.make_async_copy(inc_hbm, inc_ref, sem.at[0])
-    get_inc.start()
+def local_kernel(small_ref, counts_ref, line_ref):
     row = lax.broadcasted_iota(jnp.int32, (BLK, BLK), 0)
     col = lax.broadcasted_iota(jnp.int32, (BLK, BLK), 1)
     tri = jnp.where(row <= col, 1.0, 0.0).astype(jnp.bfloat16)
     full = jnp.ones((BLK, BLK), jnp.bfloat16)
-    get_inc.wait()
-    inc = inc_ref[...].astype(jnp.float32).astype(jnp.bfloat16)
+    inc = small_ref[...]
     for k in range(4):
         mat = jnp.concatenate([full] * k + [tri], axis=0)
         part = jnp.dot(inc[:, :BLK * (k + 1)], mat, preferred_element_type=jnp.float32)
@@ -125,17 +128,23 @@
         else:
             acc[SHIFT * far:, :] += part
         for q in range(4 * far, 4 * far + 4):
-            for h in range(2):
-                for r in range(0, 12, 4):
-                    to = 8 * h + r if r < 8 else 16 + 4 * h
-                    out_ref[PLACE[q], to:to + 4, :] = acc[12 * q + r:12 * q + r + 4, 128 * h:128 * h + 128]
+            top, low = slice(12 * q, 12 * q + 8), slice(12 * q + 8, 12 * q + 12)
+            values = [acc[top, 0:128], acc[top, 128:256], jnp.concatenate([acc[low, 0:128], acc[low, 128:256]], axis=0)]
+            most = jnp.maximum(jnp.maximum(jnp.abs(values[0]), jnp.abs(values[1])), jnp.abs(values[2]))
+            most = jnp.maximum(jnp.max(most, axis=1, keepdims=True), TINY)
+            power = jnp.broadcast_to(jnp.ceil(jnp.log2(most) - LOG_TOP), (8, 128))
+            unit = jnp.exp2(-power)
+            coded = [jnp.round(v * unit) for v in values] + [power]
+            for half in range(2):
+                rows16 = jnp.concatenate(coded[2 * half:2 * half + 2], axis=0)
+                out_ref[PLACE[q], 16 * half:16 * half + 16, :] = rows16.astype(jnp.int32).astype(jnp.int16)
 
 
 def carry_kernel(recv_ref, line_ref, carry_ref, group_ref):
     sums = recv_ref[:, 12:14, 0:128].astype(jnp.float32)
     high = sums[:, 0, :].astype(jnp.bfloat16)
     low = sums[:, 1, :].astype(jnp.bfloat16)
-    span = STRIDE * lax.broadcasted_iota(jnp.int32, (SPANS, 128), 0) % SPANS
+    span = (STRIDE * lax.broadcasted_iota(jnp.int32, (SPANS, 128), 0) + FIRST) % SPANS
     mask = jnp.where(span < lax.axis_index("tm"), 1.0, 0.0).astype(jnp.bfloat16)
     dims = (((0,), (0,)), ((), ()))
     carried = 64.0 * lax.dot_general(high, mask, dims, preferred_element_type=jnp.float32)
@@ -150,9 +159,12 @@
         out_ref[:, 128 * j:128 * j + 128] = counts_ref[:, 128 * j:128 * j + 128] + carry
 
 
-def spread_kernel(back_ref, scale_ref, out_hbm, out, sems):
+def spread_kernel(back_ref, scale_ref, out_hbm, flat, out, sems):
     copies = []
     for g in range(4):
+        base = 256 * g
+        flat[base:base + 256, :] = back_ref[base:base + 256, :].astype(jnp.int32).astype(jnp.float32)
+        units = [jnp.exp2(flat[pl.ds(base + 24 + j, 8, stride=32), :]) for j in range(8)]
         for c in range(3):
             top = 32 * c + 8 * g
             scale = jnp.broadcast_to(scale_ref[top:top + 8, :], (8, 128))
@@ -160,7 +172,7 @@
                 r = 3 * k + c
                 for h in range(2):
                     sub = 8 * h + r if r < 8 else 8 + 4 * h + r
-                    tile = back_ref[pl.ds(192 * g + sub, 8, stride=24), :]
+                    tile = flat[pl.ds(base + sub, 8, stride=32), :] * units[sub % 8]
                     out[top:top + 8, 256 * k + 128 * h:256 * k + 128 * h + 128] = tile * scale
             rows = pl.ds(top, 8)
             copies.append(pltpu.make_async_copy(out.at[rows], out_hbm.at[rows], sems.at[len(copies)]))
@@ -194,15 +206,15 @@
     sds = jax.ShapeDtypeStruct
     dma = pltpu.SemaphoreType.DMA
     chip = pltpu.VMEM
-    message, strips = call(
-        pack_kernel, (sds((SPANS, ROWS, BLK), bf16), chip((TILES, 16, 128), bf16)),
+    message, strips, small = call(
+        pack_kernel, (sds((SPANS, ROWS, BLK), bf16), chip((TILES, 16, 128), bf16), chip((CELLS, STEPS), bf16)),
         (in_hbm(noise), in_hbm(increments), in_hbm(factor.reshape(TILES, 128))), in_specs=[HBM, HBM, HBM],
         scratch=[pltpu.VMEM((CELLS, STEPS), bf16), pltpu.VMEM((CELLS, STEPS), i32), pltpu.VMEM((TILES, 128), bf16),
                  pltpu.VMEM((TILES, 128), f32), pltpu.VMEM((2, SPANS * ROWS, 128), f32), dma((3,))],
     )
     received = lax.all_to_all(message, "tm", 0, 0, tiled=True, axis_index_groups=[ORDER])
     sent = call(
-        conv_kernel, sds((SPANS, 24, 128), f32), (on_chip(received), on_chip(strips)),
+        conv_kernel, sds((SPANS, 32, 128), jnp.int16), (on_chip(received), on_chip(strips)),
         scratch=[
             pltpu.VMEM((2, SHIFT + 384, 128), f32),
             pltpu.VMEM((384, FINE * BLK), bf16),
@@ -210,17 +222,15 @@
         ],
     )
     back = lax.all_to_all(sent, "tm", 0, 0, tiled=True, axis_index_groups=[ORDER])
-    local, line = call(
-        local_kernel, (sds((CELLS, STEPS), i32), sds((8, 128), f32)), (in_hbm(increments),), in_specs=[HBM],
-        scratch=[pltpu.VMEM((CELLS, STEPS), i32), dma((1,))])
+    local, line = call(local_kernel, (sds((CELLS, STEPS), i32), sds((8, 128), f32)), (small,))
     carry, group = call(carry_kernel, (sds((CELLS, 128), i32), sds((8, 128), i32)), (received, line))
     group = group + lax.ppermute(group, "cell", [(i, i ^ 1) for i in range(8)])
     others = [lax.ppermute(group, "cell", [(i, (i + 2 * k) % 8) for i in range(8)]) for k in (1, 2, 3)]
     counts = call(counts_kernel, sds((CELLS, STEPS), i32), (local, carry))
     total = group + others[0] + others[1] + others[2]
     correlated = call(
-        spread_kernel, sds((CELLS, STEPS), f32), (on_chip(back.reshape(SPANS * 24, 128)), noise_scale[:, None]),
-        out_specs=HBM, scratch=[pltpu.VMEM((CELLS, STEPS), f32), dma((12,))],
+        spread_kernel, sds((CELLS, STEPS), f32), (on_chip(back.reshape(SPANS * 32, 128)), noise_scale[:, None]),
+        out_specs=HBM, scratch=[pltpu.VMEM((SPANS * 32, 128), f32), pltpu.VMEM((CELLS, STEPS), f32), dma((12,))],
     )
     return counts, correlated, total.reshape(STEPS)
 

time: 50.7 us -> 47.8 us (0.943)
  the two profiles are of different devices: /device:TPU:36 before, /device:TPU:32 now
where the time goes in v4:
time: 47.8 us; the launch traced here: 47.5 us
  blocking collectives  20.7 us (43%)
  starting transfers between devices  12.3 us (26%)
  Pallas kernels  8.94 us (19%)
  waiting for transfers between devices  4.2 us (9%)
  between operations  0.67 us (1%)
  other arithmetic  0.6 us (1%)
    all_to_all x1, blocking collectives, steps(): lax.all_to_all(message, 'tm', 0, 0, tiled=True, axis_index_groups=[ORDER])  20.7 us
    pallas_call x6, Pallas kernels, call(): pl.pallas_call(kernel, out_shape=outs, in_specs=in_specs or [ON_CHIP] * l...  8.94 us
    all_to_all x1, starting transfers between devices, steps(): lax.all_to_all(sent, 'tm', 0, 0, tiled=True, axis_index_groups=[ORDER])  7.76 us
    ppermute x3, starting transfers between devices, steps(): lax.ppermute(group, 'cell', [(i, (i + 2 * k) % 8) for i in range(8)])  4.44 us
    ppermute x3, waiting for transfers between devices, steps(): lax.ppermute(group, 'cell', [(i, (i + 2 * k) % 8) for i in range(8)])  3.04 us
    ppermute x1, waiting for transfers between devices, steps(): group = group + lax.ppermute(group, 'cell', [(i, i ^ 1) for i in range(8)])  1.15 us
  transfers between devices with their start and end apart: 5, of which 3 were waited for; matrix products, arithmetic and copies ran while one was open for 1% of the time, Pallas kernels for 3%

profile of v4, /device:TPU:32, one launch (start us, length us, event | category | flops | bytes accessed | tf_op | source)
XLA Modules:
  0.0 47.5 jit_solution(6593840232096928534)
XLA Ops:
  0.6 1.6 %shard_map.67 = (bf16[32,16,256]{2,1,0:T(8,128)(2,1)S(1)}, bf16[256,16,128]{2,1,0:T(8,128)(2,1)S(1)}, bf16[96,1024]{1,0:T(8,128)(2,1)S(1)}) custom-call(bf16[96,1024]{1,0:T(8,128)(2,1)} %noise_hbm.1, s32[96,1024]{1,0:T(8,128)} %inc_hbm.1, bf16[256,128]{1,0:T(8,128)(2,1)} %bitcast.6), custom_call_target="tpu_custom_call" | custom-call | tf_op jit(solution)/shard_map/pallas_call | solution.py:185
  2.2 20.7 %all_to_all.10.recv_ref = bf16[32,16,256]{2,1,0:T(8,128)(2,1)S(1)} all-to-all(bf16[32,16,256]{2,1,0:T(8,128)(2,1)S(1)} %get-tuple-element.12), channel_id=1, replica_groups={{248,32,72,112,152,192,232,16,56,96,136,176,216,0,40,80,120,160,200,240..., dimensions={0} | all-to-all | bytes 524288 | tf_op jit(solution)/shard_map/all_to_all | solution.py:215
  23.0 5.0 %shard_map.71 = s16[32,32,128]{2,1,0:T(8,128)(2,1)} custom-call(bf16[32,16,256]{2,1,0:T(8,128)(2,1)S(1)} %all_to_all.10.recv_ref, bf16[256,16,128]{2,1,0:T(8,128)(2,1)S(1)} %get-tuple-element.15.strip), custom_call_target="tpu_custom_call" | custom-call | tf_op jit(solution)/shard_map/pallas_call | solution.py:185
  28.0 7.8 %all-to-all-start.1 = ((s16[32,32,128]{2,1,0:T(8,128)(2,1)}), s16[32,32,128]{2,1,0:T(8,128)(2,1)S(1)}, u32[]{:S(2)}, u32[]{:S(2)}) async-start(s16[32,32,128]{2,1,0:T(8,128)(2,1)} %shard_map.71), calls=%async_computation.1 | async-start | bytes 524288 | tf_op jit(solution)/shard_map/all_to_all | solution.py:224
  35.7 0.3 shard_map.68
  36.0 0.2 shard_map.69
  36.3 0.1 collective-permute-start
  36.4 1.2 %collective-permute-done = s32[8,128]{1,0:T(8,128)S(1)} collective-permute-done((s32[8,128]{1,0:T(8,128)S(1)}, s32[8,128]{1,0:T(8,128)S(1)}, u32[]{:S(2)}, u32[]{:S(2)}) %collective-permute-start) | collective-permute-done | bytes 4128 | tf_op jit(solution)/shard_map/ppermute | solution.py:227
  37.5 0.0 copy-start
  37.5 2.8 %collective-permute-start.3 = (s32[8,128]{1,0:T(8,128)S(1)}, s32[8,128]{1,0:T(8,128)S(1)}, u32[]{:S(2)}, u32[]{:S(2)}) collective-permute-start(s32[8,128]{1,0:T(8,128)S(1)} %add.12), channel_id=1, source_target_pairs={{0,6},{1,7},{2,0},{3,1},{4,2},{5,3},{6,4},{7,5},{8,14},{9,15},{10,... | collective-permute-start | bytes 12296 | tf_op jit(solution)/shard_map/ppermute | solution.py:228
  40.3 0.8 %collective-permute-start.2 = (s32[8,128]{1,0:T(8,128)S(1)}, s32[8,128]{1,0:T(8,128)S(1)}, u32[]{:S(2)}, u32[]{:S(2)}) collective-permute-start(s32[8,128]{1,0:T(8,128)S(1)} %add.12), channel_id=1, source_target_pairs={{0,4},{1,5},{2,6},{3,7},{4,0},{5,1},{6,2},{7,3},{8,12},{9,13},{10,... | collective-permute-start | bytes 12296 | tf_op jit(solution)/shard_map/ppermute | solution.py:228
  41.1 0.9 %collective-permute-start.1 = (s32[8,128]{1,0:T(8,128)S(1)}, s32[8,128]{1,0:T(8,128)S(1)}, u32[]{:S(2)}, u32[]{:S(2)}) collective-permute-start(s32[8,128]{1,0:T(8,128)S(1)} %add.12), channel_id=1, source_target_pairs={{0,2},{1,3},{2,4},{3,5},{4,6},{5,7},{6,0},{7,1},{8,10},{9,11},{10,... | collective-permute-start | bytes 12296 | tf_op jit(solution)/shard_map/ppermute | solution.py:228
  42.0 0.0 copy-done
  42.0 0.1 copy.7.scale_ref
  42.1 0.8 %shard_map.70 = s32[96,1024]{1,0:T(8,128)} custom-call(s32[96,1024]{1,0:T(8,128)S(1)} %get-tuple-element.11.counts_ref, s32[96,128]{1,0:T(8,128)S(1)} %get-tuple-element.14.carry_ref), custom_call_target="tpu_custom_call" | custom-call | tf_op jit(solution)/shard_map/pallas_call | solution.py:185
  42.9 0.0 collective-permute-done.3
  42.9 2.5 %collective-permute-done.2 = s32[8,128]{1,0:T(8,128)S(1)} collective-permute-done((s32[8,128]{1,0:T(8,128)S(1)}, s32[8,128]{1,0:T(8,128)S(1)}, u32[]{:S(2)}, u32[]{:S(2)}) %collective-permute-start.2) | collective-permute-done | bytes 4128 | tf_op jit(solution)/shard_map/ppermute | solution.py:228
  45.4 0.5 %collective-permute-done.1 = s32[8,128]{1,0:T(8,128)S(1)} collective-permute-done((s32[8,128]{1,0:T(8,128)S(1)}, s32[8,128]{1,0:T(8,128)S(1)}, u32[]{:S(2)}, u32[]{:S(2)}) %collective-permute-start.1) | collective-permute-done | bytes 4128 | tf_op jit(solution)/shard_map/ppermute | solution.py:228
  45.9 0.6 %add_bitcast_fusion = s32[1024]{0:T(1024)} fusion(s32[8,128]{1,0:T(8,128)S(1)} %collective-permute-done.3, s32[8,128]{1,0:T(8,128)S(1)} %collective-permute-done.2, s32[8,128]{1,0:T(8,128)S(1)} %add.12, s32[8,128]{1,0:T(8,128)S(1)} %collective-permute-done.1), kind=kLoop, calls=%fused_computation | loop fusion | flops 3072 | bytes 20480 | tf_op jit(solution)/shard_map/reshape | solution.py:235
  46.5 0.0 all-to-all-done.1
  46.5 1.0 %shard_map.72 = f32[96,1024]{1,0:T(8,128)} custom-call(s16[1024,128]{1,0:T(8,128)(2,1)S(1)} %bitcast.5, f32[96,1]{1,0:T(8,128)S(1)} %copy.7.scale_ref), custom_call_target="tpu_custom_call" | custom-call | tf_op jit(solution)/shard_map/pallas_call | solution.py:185
  (1 shorter events, 0.0 us)
Async XLA Ops:
  28.0 18.5 %all-to-all-start.1 = ((s16[32,32,128]{2,1,0:T(8,128)(2,1)}), s16[32,32,128]{2,1,0:T(8,128)(2,1)S(1)}, u32[]{:S(2)}, u32[]{:S(2)}) async-start(s16[32,32,128]{2,1,0:T(8,128)(2,1)} %shard_map.71), calls=%async_computation.1 | async-start | bytes 524288 | tf_op jit(solution)/shard_map/all_to_all | solution.py:224
  36.3 1.2 %collective-permute-start = (s32[8,128]{1,0:T(8,128)S(1)}, s32[8,128]{1,0:T(8,128)S(1)}, u32[]{:S(2)}, u32[]{:S(2)}) collective-permute-start(s32[8,128]{1,0:T(8,128)S(1)} %get-tuple-element.16), channel_id=1, source_target_pairs={{0,1},{1,0},{2,3},{3,2},{4,5},{5,4},{6,7},{7,6},{8,9},{9,8},{10,11... | collective-permute-start | bytes 12296 | tf_op jit(solution)/shard_map/ppermute | solution.py:227
  37.5 4.4 %copy-start = (f32[96]{0:T(128)S(1)}, f32[96]{0:T(128)}, u32[]{:S(2)}) copy-start(f32[96]{0:T(128)} %param.6) | copy-start | bytes 1156
  37.5 5.3 %collective-permute-start.3 = (s32[8,128]{1,0:T(8,128)S(1)}, s32[8,128]{1,0:T(8,128)S(1)}, u32[]{:S(2)}, u32[]{:S(2)}) collective-permute-start(s32[8,128]{1,0:T(8,128)S(1)} %add.12), channel_id=1, source_target_pairs={{0,6},{1,7},{2,0},{3,1},{4,2},{5,3},{6,4},{7,5},{8,14},{9,15},{10,... | collective-permute-start | bytes 12296 | tf_op jit(solution)/shard_map/ppermute | solution.py:228
  40.3 5.1 %collective-permute-start.2 = (s32[8,128]{1,0:T(8,128)S(1)}, s32[8,128]{1,0:T(8,128)S(1)}, u32[]{:S(2)}, u32[]{:S(2)}) collective-permute-start(s32[8,128]{1,0:T(8,128)S(1)} %add.12), channel_id=1, source_target_pairs={{0,4},{1,5},{2,6},{3,7},{4,0},{5,1},{6,2},{7,3},{8,12},{9,13},{10,... | collective-permute-start | bytes 12296 | tf_op jit(solution)/shard_map/ppermute | solution.py:228
  41.1 4.8 %collective-permute-start.1 = (s32[8,128]{1,0:T(8,128)S(1)}, s32[8,128]{1,0:T(8,128)S(1)}, u32[]{:S(2)}, u32[]{:S(2)}) collective-permute-start(s32[8,128]{1,0:T(8,128)S(1)} %add.12), channel_id=1, source_target_pairs={{0,2},{1,3},{2,4},{3,5},{4,6},{5,7},{6,0},{7,1},{8,10},{9,11},{10,... | collective-permute-start | bytes 12296 | tf_op jit(solution)/shard_map/ppermute | solution.py:228

commit v5 on v4

--- a/solution.py
+++ b/solution.py
@@ -17,9 +17,13 @@
 SHIFT = 3 * FINE
 LOG_TOP = math.log2(32000.0)
 TINY = 2.0 ** -100
-STRIDE = 5
-FIRST = 31
-ORDER = [(STRIDE * p + FIRST) % SPANS for p in range(SPANS)]
+
+
+def member(place):
+    return place % 4 * 8 + 7 - place // 4
+
+
+ORDER = [member(p) for p in range(SPANS)]
 PLACE = [ORDER.index(q) for q in range(SPANS)]
 FAR = 128 // FINE
 
@@ -27,13 +31,15 @@
 HBM = pl.BlockSpec(memory_space=pltpu.HBM)
 
 
-def pack_kernel(noise_hbm, inc_hbm, factor_hbm, out, strip_ref, small_ref, x_ref, inc_ref, factor_ref, lines, scr, sems):
+def pack_kernel(noise_hbm, inc_hbm, factor_hbm, scale_hbm, out, strip_ref, small_ref, scale_ref, x_ref, inc_ref, factor_ref, lines, scr, sems):
     get_noise = pltpu.make_async_copy(noise_hbm, x_ref, sems.at[0])
     get_inc = pltpu.make_async_copy(inc_hbm, inc_ref, sems.at[1])
     get_factor = pltpu.make_async_copy(factor_hbm, factor_ref, sems.at[2])
+    get_scale = pltpu.make_async_copy(scale_hbm, scale_ref, sems.at[3])
     get_factor.start()
     get_inc.start()
     get_noise.start()
+    get_scale.start()
 
     get_factor.wait()
     lines[...] = factor_ref[...].astype(jnp.float32)
@@ -57,6 +63,7 @@
     low = sums - 64.0 * high
     zero = jnp.zeros((8, 128), jnp.float32)
     get_noise.wait()
+    get_scale.wait()
     for g in range(4):
         base = 8 * g * ROWS
         for h in range(2):
@@ -72,19 +79,14 @@
             out[8 * g:8 * g + 8, :, 128 * h:128 * h + 128] = tile.reshape(8, ROWS, 128)
 
 
-def local_kernel(small_ref, counts_ref, line_ref):
+def running(inc):
     row = lax.broadcasted_iota(jnp.int32, (BLK, BLK), 0)
     col = lax.broadcasted_iota(jnp.int32, (BLK, BLK), 1)
     tri = jnp.where(row <= col, 1.0, 0.0).astype(jnp.bfloat16)
     full = jnp.ones((BLK, BLK), jnp.bfloat16)
-    inc = small_ref[...]
     for k in range(4):
         mat = jnp.concatenate([full] * k + [tri], axis=0)
-        part = jnp.dot(inc[:, :BLK * (k + 1)], mat, preferred_element_type=jnp.float32)
-        counts_ref[:, BLK * k:BLK * (k + 1)] = part.astype(jnp.int32)
-        total = jnp.sum(part, axis=0, keepdims=True)
-        for h in range(2):
-            line_ref[2 * k + h:2 * k + h + 1, :] = total[:, 128 * h:128 * h + 128]
+        yield k, jnp.dot(inc[:, :BLK * (k + 1)], mat, preferred_element_type=jnp.float32)
 
 
 def conv_kernel(recv_ref, strip, out_ref, xf, xs, acc):
@@ -140,34 +142,43 @@
                 out_ref[PLACE[q], 16 * half:16 * half + 16, :] = rows16.astype(jnp.int32).astype(jnp.int16)
 
 
-def carry_kernel(recv_ref, line_ref, carry_ref, group_ref):
+def carry_kernel(recv_ref, small_ref, scale_ref, carry_ref, group_ref, wide_ref):
     sums = recv_ref[:, 12:14, 0:128].astype(jnp.float32)
     high = sums[:, 0, :].astype(jnp.bfloat16)
     low = sums[:, 1, :].astype(jnp.bfloat16)
-    span = (STRIDE * lax.broadcasted_iota(jnp.int32, (SPANS, 128), 0) + FIRST) % SPANS
-    mask = jnp.where(span < lax.axis_index("tm"), 1.0, 0.0).astype(jnp.bfloat16)
+    place = lax.broadcasted_iota(jnp.int32, (SPANS, 128), 0)
+    mask = jnp.where(member(place) < lax.axis_index("tm"), 1.0, 0.0).astype(jnp.bfloat16)
     dims = (((0,), (0,)), ((), ()))
     carried = 64.0 * lax.dot_general(high, mask, dims, preferred_element_type=jnp.float32)
     carried = (carried + lax.dot_general(low, mask, dims, preferred_element_type=jnp.float32))[:CELLS]
     carry_ref[...] = carried.astype(jnp.int32)
-    group_ref[...] = (line_ref[...] + jnp.sum(carried, axis=0, keepdims=True)).astype(jnp.int32)
-
-
-def counts_kernel(counts_ref, carry_ref, out_ref):
+    before = jnp.sum(carried, axis=0, keepdims=True)
+    for k, part in running(small_ref[...]):
+        total = jnp.sum(part, axis=0, keepdims=True)
+        for h in range(2):
+            group_ref[2 * k + h:2 * k + h + 1, :] = (total[:, 128 * h:128 * h + 128] + before).astype(jnp.int32)
+    wide_ref[...] = jnp.transpose(jnp.broadcast_to(scale_ref[...], (128, CELLS)))
+
+
+def counts_kernel(small_ref, carry_ref, out_ref):
     carry = carry_ref[...]
-    for j in range(8):
-        out_ref[:, 128 * j:128 * j + 128] = counts_ref[:, 128 * j:128 * j + 128] + carry
-
-
-def spread_kernel(back_ref, scale_ref, out_hbm, flat, out, sems):
-    copies = []
+    for k, part in running(small_ref[...]):
+        for h in range(2):
+            lane = BLK * k + 128 * h
+            out_ref[:, lane:lane + 128] = part[:, 128 * h:128 * h + 128].astype(jnp.int32) + carry
+
+
+def spread_kernel(back_ref, scale_ref, group_ref, other_ref, out_hbm, total_hbm, flat, out, total, sems):
+    total[...] = group_ref[...] + other_ref[...]
+    copies = [pltpu.make_async_copy(total, total_hbm, sems.at[0])]
+    copies[0].start()
     for g in range(4):
         base = 256 * g
         flat[base:base + 256, :] = back_ref[base:base + 256, :].astype(jnp.int32).astype(jnp.float32)
         units = [jnp.exp2(flat[pl.ds(base + 24 + j, 8, stride=32), :]) for j in range(8)]
         for c in range(3):
             top = 32 * c + 8 * g
-            scale = jnp.broadcast_to(scale_ref[top:top + 8, :], (8, 128))
+            scale = scale_ref[top:top + 8, :]
             for k in range(4):
                 r = 3 * k + c
                 for h in range(2):
@@ -206,11 +217,12 @@
     sds = jax.ShapeDtypeStruct
     dma = pltpu.SemaphoreType.DMA
     chip = pltpu.VMEM
-    message, strips, small = call(
-        pack_kernel, (sds((SPANS, ROWS, BLK), bf16), chip((TILES, 16, 128), bf16), chip((CELLS, STEPS), bf16)),
-        (in_hbm(noise), in_hbm(increments), in_hbm(factor.reshape(TILES, 128))), in_specs=[HBM, HBM, HBM],
+    message, strips, small, scales = call(
+        pack_kernel, (sds((SPANS, ROWS, BLK), bf16), chip((TILES, 16, 128), bf16), chip((CELLS, STEPS), bf16), chip((1, CELLS), f32)),
+        (in_hbm(noise), in_hbm(increments), in_hbm(factor.reshape(TILES, 128)), in_hbm(noise_scale.reshape(1, CELLS))),
+        in_specs=[HBM] * 4,
         scratch=[pltpu.VMEM((CELLS, STEPS), bf16), pltpu.VMEM((CELLS, STEPS), i32), pltpu.VMEM((TILES, 128), bf16),
-                 pltpu.VMEM((TILES, 128), f32), pltpu.VMEM((2, SPANS * ROWS, 128), f32), dma((3,))],
+                 pltpu.VMEM((TILES, 128), f32), pltpu.VMEM((2, SPANS * ROWS, 128), f32), dma((4,))],
     )
     received = lax.all_to_all(message, "tm", 0, 0, tiled=True, axis_index_groups=[ORDER])
     sent = call(
@@ -222,15 +234,18 @@
         ],
     )
     back = lax.all_to_all(sent, "tm", 0, 0, tiled=True, axis_index_groups=[ORDER])
-    local, line = call(local_kernel, (sds((CELLS, STEPS), i32), sds((8, 128), f32)), (small,))
-    carry, group = call(carry_kernel, (sds((CELLS, 128), i32), sds((8, 128), i32)), (received, line))
+    carry, group, wide = call(
+        carry_kernel, (sds((CELLS, 128), i32), sds((8, 128), i32), chip((CELLS, 128), f32)),
+        (received, small, on_chip(scales)))
     group = group + lax.ppermute(group, "cell", [(i, i ^ 1) for i in range(8)])
-    others = [lax.ppermute(group, "cell", [(i, (i + 2 * k) % 8) for i in range(8)]) for k in (1, 2, 3)]
-    counts = call(counts_kernel, sds((CELLS, STEPS), i32), (local, carry))
-    total = group + others[0] + others[1] + others[2]
-    correlated = call(
-        spread_kernel, sds((CELLS, STEPS), f32), (on_chip(back.reshape(SPANS * 32, 128)), noise_scale[:, None]),
-        out_specs=HBM, scratch=[pltpu.VMEM((SPANS * 32, 128), f32), pltpu.VMEM((CELLS, STEPS), f32), dma((12,))],
+    group = group + lax.ppermute(group, "cell", [(i, i ^ 2) for i in range(8)])
+    other = lax.ppermute(group, "cell", [(i, i ^ 6) for i in range(8)])
+    counts = call(counts_kernel, sds((CELLS, STEPS), i32), (small, carry))
+    correlated, total = call(
+        spread_kernel, (sds((CELLS, STEPS), f32), sds((8, 128), i32)),
+        (on_chip(back.reshape(SPANS * 32, 128)), on_chip(wide), on_chip(group), on_chip(other)),
+        out_specs=(HBM, HBM),
+        scratch=[pltpu.VMEM((SPANS * 32, 128), f32), pltpu.VMEM((CELLS, STEPS), f32), pltpu.VMEM((8, 128), i32), dma((13,))],
     )
     return counts, correlated, total.reshape(STEPS)
 

time: 47.8 us -> 47.1 us (0.985)
  the two profiles are of different devices: /device:TPU:32 before, /device:TPU:6 now
where the time goes in v5:
time: 47.1 us; the launch traced here: 46.9 us
  blocking collectives  22 us (47%)
  Pallas kernels  9.09 us (19%)
  starting transfers between devices  7.86 us (17%)
  waiting for transfers between devices  7.23 us (15%)
  between operations  0.67 us (1%)
    all_to_all x1, blocking collectives, steps(): lax.all_to_all(message, 'tm', 0, 0, tiled=True, axis_index_groups=[ORDER])  22 us
    pallas_call x5, Pallas kernels, call(): pl.pallas_call(kernel, out_shape=outs, in_specs=in_specs or [ON_CHIP] * l...  9.09 us
    all_to_all x1, starting transfers between devices, steps(): lax.all_to_all(sent, 'tm', 0, 0, tiled=True, axis_index_groups=[ORDER])  6.46 us
    ppermute x1, waiting for transfers between devices, steps(): other = lax.ppermute(group, 'cell', [(i, i ^ 6) for i in range(8)])  3.3 us
    ppermute x1, waiting for transfers between devices, steps(): group = group + lax.ppermute(group, 'cell', [(i, i ^ 2) for i in range(8)])  2.78 us
    ppermute x1, waiting for transfers between devices, steps(): group = group + lax.ppermute(group, 'cell', [(i, i ^ 1) for i in range(8)])  1.15 us
  transfers between devices with their start and end apart: 4, of which 3 were waited for; matrix products, arithmetic and copies ran while one was open for 0% of the time, Pallas kernels for 3%

profile of v5, /device:TPU:6, one launch (start us, length us, event | category | flops | bytes accessed | tf_op | source)
XLA Modules:
  0.0 46.9 jit_solution(8807811347884306603)
XLA Ops:
  0.6 1.6 %shard_map.67 = (bf16[32,16,256]{2,1,0:T(8,128)(2,1)S(1)}, bf16[256,16,128]{2,1,0:T(8,128)(2,1)S(1)}, bf16[96,1024]{1,0:T(8,128)(2,1)S(1)}, f32[1,96]{1,0:T(1,128)S(1)}) custom-call(bf16[96,1024]{1,0:T(8,128)(2,1)} %noise_hbm.1, s32[96,1024]{1,0:T(8,128)} %inc_hbm.1, bf16[256,128]{1,0:T(8,128)(2,1)} %bitcast.5, f32[1,96]{1,0:T(1,128)} %bitcast.6), custom_call_target="tpu_custom_call" | custom-call | tf_op jit(solution)/shard_map/pallas_call | solution.py:196
  2.2 22.0 %all_to_all.10.recv_ref = bf16[32,16,256]{2,1,0:T(8,128)(2,1)S(1)} all-to-all(bf16[32,16,256]{2,1,0:T(8,128)(2,1)S(1)} %get-tuple-element.13), channel_id=1, replica_groups={{56,120,184,248,48,112,176,240,40,104,168,232,32,96,160,224,24,88,152,2..., dimensions={0} | all-to-all | bytes 524288 | tf_op jit(solution)/shard_map/all_to_all | solution.py:227
  24.2 5.0 %shard_map.70 = s16[32,32,128]{2,1,0:T(8,128)(2,1)} custom-call(bf16[32,16,256]{2,1,0:T(8,128)(2,1)S(1)} %all_to_all.10.recv_ref, bf16[256,16,128]{2,1,0:T(8,128)(2,1)S(1)} %get-tuple-element.16.strip), custom_call_target="tpu_custom_call" | custom-call | tf_op jit(solution)/shard_map/pallas_call | solution.py:196
  29.2 6.5 %all-to-all-start.1 = ((s16[32,32,128]{2,1,0:T(8,128)(2,1)}), s16[32,32,128]{2,1,0:T(8,128)(2,1)S(1)}, u32[]{:S(2)}, u32[]{:S(2)}) async-start(s16[32,32,128]{2,1,0:T(8,128)(2,1)} %shard_map.70), calls=%async_computation.1 | async-start | bytes 524288 | tf_op jit(solution)/shard_map/all_to_all | solution.py:236
  35.7 0.4 shard_map.68
  36.1 0.1 collective-permute-start
  36.2 1.2 %collective-permute-done = s32[8,128]{1,0:T(8,128)S(1)} collective-permute-done((s32[8,128]{1,0:T(8,128)S(1)}, s32[8,128]{1,0:T(8,128)S(1)}, u32[]{:S(2)}, u32[]{:S(2)}) %collective-permute-start) | collective-permute-done | bytes 4128 | tf_op jit(solution)/shard_map/ppermute | solution.py:240
  37.4 0.8 %collective-permute-start.1 = (s32[8,128]{1,0:T(8,128)S(1)}, s32[8,128]{1,0:T(8,128)S(1)}, u32[]{:S(2)}, u32[]{:S(2)}) collective-permute-start(s32[8,128]{1,0:T(8,128)S(1)} %add.6), channel_id=1, source_target_pairs={{0,2},{1,3},{2,0},{3,1},{4,6},{5,7},{6,4},{7,5},{8,10},{9,11},{10,... | collective-permute-start | bytes 12296 | tf_op jit(solution)/shard_map/ppermute | solution.py:241
  38.2 2.8 %collective-permute-done.1 = s32[8,128]{1,0:T(8,128)S(1)} collective-permute-done((s32[8,128]{1,0:T(8,128)S(1)}, s32[8,128]{1,0:T(8,128)S(1)}, u32[]{:S(2)}, u32[]{:S(2)}) %collective-permute-start.1) | collective-permute-done | bytes 4128 | tf_op jit(solution)/shard_map/ppermute | solution.py:241
  41.0 0.5 %collective-permute-start.2 = (s32[8,128]{1,0:T(8,128)S(1)}, s32[8,128]{1,0:T(8,128)S(1)}, u32[]{:S(2)}, u32[]{:S(2)}) collective-permute-start(s32[8,128]{1,0:T(8,128)S(1)} %add.7.group_ref), channel_id=1, source_target_pairs={{0,6},{1,7},{2,4},{3,5},{4,2},{5,3},{6,0},{7,1},{8,14},{9,15},{10,... | collective-permute-start | bytes 12296 | tf_op jit(solution)/shard_map/ppermute | solution.py:242
  41.4 1.0 %shard_map.69 = s32[96,1024]{1,0:T(8,128)} custom-call(bf16[96,1024]{1,0:T(8,128)(2,1)S(1)} %get-tuple-element.12.small_ref, s32[96,128]{1,0:T(8,128)S(1)} %get-tuple-element.15.carry_ref), custom_call_target="tpu_custom_call" | custom-call | tf_op jit(solution)/shard_map/pallas_call | solution.py:196
  42.5 3.3 %collective-permute-done.2.other_ref = s32[8,128]{1,0:T(8,128)S(1)} collective-permute-done((s32[8,128]{1,0:T(8,128)S(1)}, s32[8,128]{1,0:T(8,128)S(1)}, u32[]{:S(2)}, u32[]{:S(2)}) %collective-permute-start.2) | collective-permute-done | bytes 4128 | tf_op jit(solution)/shard_map/ppermute | solution.py:242
  45.8 0.0 all-to-all-done.1
  45.8 1.1 %shard_map.71 = (f32[96,1024]{1,0:T(8,128)}, s32[8,128]{1,0:T(8,128)}) custom-call(s16[1024,128]{1,0:T(8,128)(2,1)S(1)} %bitcast.4, f32[96,128]{1,0:T(8,128)S(1)} %get-tuple-element.17.scale_ref, s32[8,128]{1,0:T(8,128)S(1)} %add.7.group_ref, s32[8,128]{1,0:T(8,128)S(1)} %collective-permute-done.2.other_ref), custom_call_target="tpu_custom_call" | custom-call | tf_op jit(solution)/shard_map/pallas_call | solution.py:196
  (2 shorter events, 0.0 us)
Async XLA Ops:
  29.2 16.6 %all-to-all-start.1 = ((s16[32,32,128]{2,1,0:T(8,128)(2,1)}), s16[32,32,128]{2,1,0:T(8,128)(2,1)S(1)}, u32[]{:S(2)}, u32[]{:S(2)}) async-start(s16[32,32,128]{2,1,0:T(8,128)(2,1)} %shard_map.70), calls=%async_computation.1 | async-start | bytes 524288 | tf_op jit(solution)/shard_map/all_to_all | solution.py:236
  36.1 1.3 %collective-permute-start = (s32[8,128]{1,0:T(8,128)S(1)}, s32[8,128]{1,0:T(8,128)S(1)}, u32[]{:S(2)}, u32[]{:S(2)}) collective-permute-start(s32[8,128]{1,0:T(8,128)S(1)} %get-tuple-element.18), channel_id=1, source_target_pairs={{0,1},{1,0},{2,3},{3,2},{4,5},{5,4},{6,7},{7,6},{8,9},{9,8},{10,11... | collective-permute-start | bytes 12296 | tf_op jit(solution)/shard_map/ppermute | solution.py:240
  37.4 3.6 %collective-permute-start.1 = (s32[8,128]{1,0:T(8,128)S(1)}, s32[8,128]{1,0:T(8,128)S(1)}, u32[]{:S(2)}, u32[]{:S(2)}) collective-permute-start(s32[8,128]{1,0:T(8,128)S(1)} %add.6), channel_id=1, source_target_pairs={{0,2},{1,3},{2,0},{3,1},{4,6},{5,7},{6,4},{7,5},{8,10},{9,11},{10,... | collective-permute-start | bytes 12296 | tf_op jit(solution)/shard_map/ppermute | solution.py:241
  41.0 4.8 %collective-permute-start.2 = (s32[8,128]{1,0:T(8,128)S(1)}, s32[8,128]{1,0:T(8,128)S(1)}, u32[]{:S(2)}, u32[]{:S(2)}) collective-permute-start(s32[8,128]{1,0:T(8,128)S(1)} %add.7.group_ref), channel_id=1, source_target_pairs={{0,6},{1,7},{2,4},{3,5},{4,2},{5,3},{6,0},{7,1},{8,14},{9,15},{10,... | collective-permute-start | bytes 12296 | tf_op jit(solution)/shard_map/ppermute | solution.py:242

commit v6 on v5

--- a/solution.py
+++ b/solution.py
@@ -13,14 +13,14 @@
 BLK = 256
 ROWS = 16
 TILES = 256
-FINE = 16
+FINE = 8
 SHIFT = 3 * FINE
 LOG_TOP = math.log2(32000.0)
 TINY = 2.0 ** -100
 
 
 def member(place):
-    return place % 4 * 8 + 7 - place // 4
+    return place % 4 * 8 + (place // 4 + 7) % 8
 
 
 ORDER = [member(p) for p in range(SPANS)]
@@ -129,7 +129,7 @@
             acc[...] = part
         else:
             acc[SHIFT * far:, :] += part
-        for q in range(4 * far, 4 * far + 4):
+        for q in range(SPANS // FAR * far, SPANS // FAR * (far + 1)):
             top, low = slice(12 * q, 12 * q + 8), slice(12 * q + 8, 12 * q + 12)
             values = [acc[top, 0:128], acc[top, 128:256], jnp.concatenate([acc[low, 0:128], acc[low, 128:256]], axis=0)]
             most = jnp.maximum(jnp.maximum(jnp.abs(values[0]), jnp.abs(values[1])), jnp.abs(values[2]))

time: 47.1 us -> 46.8 us (level)
  no operation moved by 1% of the time
where the time goes in v6:
time: 46.8 us; the launch traced here: 46.6 us
  blocking collectives  22.3 us (48%)
  Pallas kernels  8.96 us (19%)
  starting transfers between devices  7.47 us (16%)
  waiting for transfers between devices  7.23 us (15%)
  between operations  0.67 us (1%)
    all_to_all x1, blocking collectives, steps(): lax.all_to_all(message, 'tm', 0, 0, tiled=True, axis_index_groups=[ORDER])  22.3 us
    pallas_call x5, Pallas kernels, call(): pl.pallas_call(kernel, out_shape=outs, in_specs=in_specs or [ON_CHIP] * l...  8.96 us
    all_to_all x1, starting transfers between devices, steps(): lax.all_to_all(sent, 'tm', 0, 0, tiled=True, axis_index_groups=[ORDER])  6.07 us
    ppermute x1, waiting for transfers between devices, steps(): other = lax.ppermute(group, 'cell', [(i, i ^ 6) for i in range(8)])  3.3 us
    ppermute x1, waiting for transfers between devices, steps(): group = group + lax.ppermute(group, 'cell', [(i, i ^ 2) for i in range(8)])  2.78 us
    ppermute x1, waiting for transfers between devices, steps(): group = group + lax.ppermute(group, 'cell', [(i, i ^ 1) for i in range(8)])  1.15 us
  transfers between devices with their start and end apart: 4, of which 3 were waited for; matrix products, arithmetic and copies ran while one was open for 0% of the time, Pallas kernels for 3%

profile of v6, /device:TPU:6, one launch (start us, length us, event | category | flops | bytes accessed | tf_op | source)
XLA Modules:
  0.0 46.6 jit_solution(9386079527444363530)
XLA Ops:
  0.6 1.6 %shard_map.67 = (bf16[32,16,256]{2,1,0:T(8,128)(2,1)S(1)}, bf16[256,16,128]{2,1,0:T(8,128)(2,1)S(1)}, bf16[96,1024]{1,0:T(8,128)(2,1)S(1)}, f32[1,96]{1,0:T(1,128)S(1)}) custom-call(bf16[96,1024]{1,0:T(8,128)(2,1)} %noise_hbm.1, s32[96,1024]{1,0:T(8,128)} %inc_hbm.1, bf16[256,128]{1,0:T(8,128)(2,1)} %bitcast.5, f32[1,96]{1,0:T(1,128)} %bitcast.6), custom_call_target="tpu_custom_call" | custom-call | tf_op jit(solution)/shard_map/pallas_call | solution.py:196
  2.2 22.3 %all_to_all.10.recv_ref = bf16[32,16,256]{2,1,0:T(8,128)(2,1)S(1)} all-to-all(bf16[32,16,256]{2,1,0:T(8,128)(2,1)S(1)} %get-tuple-element.13), channel_id=1, replica_groups={{56,120,184,248,0,64,128,192,8,72,136,200,16,80,144,208,24,88,152,216,3..., dimensions={0} | all-to-all | bytes 524288 | tf_op jit(solution)/shard_map/all_to_all | solution.py:227
  24.5 4.9 %shard_map.70 = s16[32,32,128]{2,1,0:T(8,128)(2,1)} custom-call(bf16[32,16,256]{2,1,0:T(8,128)(2,1)S(1)} %all_to_all.10.recv_ref, bf16[256,16,128]{2,1,0:T(8,128)(2,1)S(1)} %get-tuple-element.16.strip), custom_call_target="tpu_custom_call" | custom-call | tf_op jit(solution)/shard_map/pallas_call | solution.py:196
  29.4 6.1 %all-to-all-start.1 = ((s16[32,32,128]{2,1,0:T(8,128)(2,1)}), s16[32,32,128]{2,1,0:T(8,128)(2,1)S(1)}, u32[]{:S(2)}, u32[]{:S(2)}) async-start(s16[32,32,128]{2,1,0:T(8,128)(2,1)} %shard_map.70), calls=%async_computation.1 | async-start | bytes 524288 | tf_op jit(solution)/shard_map/all_to_all | solution.py:236
  35.5 0.4 shard_map.68
  35.9 0.1 collective-permute-start
  36.0 1.2 %collective-permute-done = s32[8,128]{1,0:T(8,128)S(1)} collective-permute-done((s32[8,128]{1,0:T(8,128)S(1)}, s32[8,128]{1,0:T(8,128)S(1)}, u32[]{:S(2)}, u32[]{:S(2)}) %collective-permute-start) | collective-permute-done | bytes 4128 | tf_op jit(solution)/shard_map/ppermute | solution.py:240
  37.1 0.8 %collective-permute-start.1 = (s32[8,128]{1,0:T(8,128)S(1)}, s32[8,128]{1,0:T(8,128)S(1)}, u32[]{:S(2)}, u32[]{:S(2)}) collective-permute-start(s32[8,128]{1,0:T(8,128)S(1)} %add.6), channel_id=1, source_target_pairs={{0,2},{1,3},{2,0},{3,1},{4,6},{5,7},{6,4},{7,5},{8,10},{9,11},{10,... | collective-permute-start | bytes 12296 | tf_op jit(solution)/shard_map/ppermute | solution.py:241
  37.9 2.8 %collective-permute-done.1 = s32[8,128]{1,0:T(8,128)S(1)} collective-permute-done((s32[8,128]{1,0:T(8,128)S(1)}, s32[8,128]{1,0:T(8,128)S(1)}, u32[]{:S(2)}, u32[]{:S(2)}) %collective-permute-start.1) | collective-permute-done | bytes 4128 | tf_op jit(solution)/shard_map/ppermute | solution.py:241
  40.7 0.5 %collective-permute-start.2 = (s32[8,128]{1,0:T(8,128)S(1)}, s32[8,128]{1,0:T(8,128)S(1)}, u32[]{:S(2)}, u32[]{:S(2)}) collective-permute-start(s32[8,128]{1,0:T(8,128)S(1)} %add.7.group_ref), channel_id=1, source_target_pairs={{0,6},{1,7},{2,4},{3,5},{4,2},{5,3},{6,0},{7,1},{8,14},{9,15},{10,... | collective-permute-start | bytes 12296 | tf_op jit(solution)/shard_map/ppermute | solution.py:242
  41.2 1.0 %shard_map.69 = s32[96,1024]{1,0:T(8,128)} custom-call(bf16[96,1024]{1,0:T(8,128)(2,1)S(1)} %get-tuple-element.12.small_ref, s32[96,128]{1,0:T(8,128)S(1)} %get-tuple-element.15.carry_ref), custom_call_target="tpu_custom_call" | custom-call | tf_op jit(solution)/shard_map/pallas_call | solution.py:196
  42.2 3.3 %collective-permute-done.2.other_ref = s32[8,128]{1,0:T(8,128)S(1)} collective-permute-done((s32[8,128]{1,0:T(8,128)S(1)}, s32[8,128]{1,0:T(8,128)S(1)}, u32[]{:S(2)}, u32[]{:S(2)}) %collective-permute-start.2) | collective-permute-done | bytes 4128 | tf_op jit(solution)/shard_map/ppermute | solution.py:242
  45.5 0.0 all-to-all-done.1
  45.5 1.1 %shard_map.71 = (f32[96,1024]{1,0:T(8,128)}, s32[8,128]{1,0:T(8,128)}) custom-call(s16[1024,128]{1,0:T(8,128)(2,1)S(1)} %bitcast.4, f32[96,128]{1,0:T(8,128)S(1)} %get-tuple-element.17.scale_ref, s32[8,128]{1,0:T(8,128)S(1)} %add.7.group_ref, s32[8,128]{1,0:T(8,128)S(1)} %collective-permute-done.2.other_ref), custom_call_target="tpu_custom_call" | custom-call | tf_op jit(solution)/shard_map/pallas_call | solution.py:196
  (2 shorter events, 0.0 us)
Async XLA Ops:
  29.4 16.2 %all-to-all-start.1 = ((s16[32,32,128]{2,1,0:T(8,128)(2,1)}), s16[32,32,128]{2,1,0:T(8,128)(2,1)S(1)}, u32[]{:S(2)}, u32[]{:S(2)}) async-start(s16[32,32,128]{2,1,0:T(8,128)(2,1)} %shard_map.70), calls=%async_computation.1 | async-start | bytes 524288 | tf_op jit(solution)/shard_map/all_to_all | solution.py:236
  35.9 1.3 %collective-permute-start = (s32[8,128]{1,0:T(8,128)S(1)}, s32[8,128]{1,0:T(8,128)S(1)}, u32[]{:S(2)}, u32[]{:S(2)}) collective-permute-start(s32[8,128]{1,0:T(8,128)S(1)} %get-tuple-element.18), channel_id=1, source_target_pairs={{0,1},{1,0},{2,3},{3,2},{4,5},{5,4},{6,7},{7,6},{8,9},{9,8},{10,11... | collective-permute-start | bytes 12296 | tf_op jit(solution)/shard_map/ppermute | solution.py:240
  37.1 3.6 %collective-permute-start.1 = (s32[8,128]{1,0:T(8,128)S(1)}, s32[8,128]{1,0:T(8,128)S(1)}, u32[]{:S(2)}, u32[]{:S(2)}) collective-permute-start(s32[8,128]{1,0:T(8,128)S(1)} %add.6), channel_id=1, source_target_pairs={{0,2},{1,3},{2,0},{3,1},{4,6},{5,7},{6,4},{7,5},{8,10},{9,11},{10,... | collective-permute-start | bytes 12296 | tf_op jit(solution)/shard_map/ppermute | solution.py:241
  40.7 4.8 %collective-permute-start.2 = (s32[8,128]{1,0:T(8,128)S(1)}, s32[8,128]{1,0:T(8,128)S(1)}, u32[]{:S(2)}, u32[]{:S(2)}) collective-permute-start(s32[8,128]{1,0:T(8,128)S(1)} %add.7.group_ref), channel_id=1, source_target_pairs={{0,6},{1,7},{2,4},{3,5},{4,2},{5,3},{6,0},{7,1},{8,14},{9,15},{10,... | collective-permute-start | bytes 12296 | tf_op jit(solution)/shard_map/ppermute | solution.py:242
